TPU v7x, 32 devices: a whole 2x2x4 slice. The times are simulated.
32 devices in a mesh: gx: 8 (over z, x), gy: 4 (over y, core).
Axes of the slice: x: 2, y: 2, z: 4, core: 2. Of those that a mesh axis runs over, the one named last changes fastest.
Arguments:
- features: bfloat16 [32, 8192], P(None, ('gx', 'gy')), may hold values from -6 to 6
- offsets: bfloat16 [3, 8192], P(None, ('gx', 'gy')), may hold values from 0 to 16
- point_cell: int32 [8192], P(('gx', 'gy')), may hold values from 0 to 31
- tile_owner: int32 [64, 4], P(('gx', 'gy')), may hold values from 0 to 3, all different within a row; in each aligned block of 2 rows (0 to 1, 2 to 3, ...) at most 2 rows name the same one
- tile_local: int32 [64, 4], P(('gx', 'gy')), may hold values from 0 to 31
- live_count: int32 [64], P(('gx', 'gy')), may hold values from 1 to 4
- w_first: bfloat16 [64, 3], replicated, may hold values from -3.5 to 3.5
- b_first: float32 [64], replicated, may hold values from -3 to 3
- w_second: bfloat16 [64, 64], replicated, may hold values from -0.75 to 0.75
- b_second: float32 [64], replicated, may hold values from -3 to 3
- w_third: bfloat16 [32, 64], replicated, may hold values from -0.75 to 0.75
- w_point: bfloat16 [32, 32], replicated, may hold values from -1 to 1
- b_point: float32 [32], replicated, may hold values from -3 to 3
- w_modes: bfloat16 [32, 32, 32, 2, 32, 32], P(None, 'gx', 'gy'), may hold values from -3 to 3
Outputs:
- latent_out: float32 [32, 32, 32, 128], P('gx', 'gy')
Inputs may be any that keep to these rules, and one draw needn't show every extreme that they name: `tile_owner`: each row names 4 different owners; among the rows of one device no owner is named by more than 2 rows.
All inputs are finite; a program needn't handle non-finite values.
Results may differ from a plain program's by a relative error of at most 0.0015.
Values may be sent and summed in bfloat16 or wider, within the bound.
A program may use at most 64 MiB of HBM per device.

v0:
```python
import math

import jax
import numpy as np
import jax.numpy as jnp
from jax import lax
from jax.experimental import pallas as pl
from jax.experimental.pallas import tpu as pltpu
from jax.sharding import PartitionSpec as P

NZ = 128
CX = 4
CY = 8
SPAN = 16
PB = 128


GROUP = 4
ROWS = 8


def pair_kernel(
    owner_ref,
    local_ref,
    live_ref,
    features_ref,
    offsets_ref,
    cells_ref,
    w_first_ref,
    b_first_ref,
    w_second_ref,
    b_second_ref,
    w_third_ref,
    table_ref,
    sent_ref,
    chunk_ref,
    cos_p,
    sin_p,
    cos_z,
    sin_z,
    flat,
    feats_ref,
    first_ref,
    second_ref,
    third_ref,
):
    blocks, listed = owner_ref.shape
    row_index = lax.axis_index("gx")
    width = second_ref.shape[0]
    hid = width // GROUP
    groups = NZ // GROUP
    scale = 1.0 / math.sqrt(PB)
    linear = 2.0 * math.sqrt(2.0 / math.pi)
    cubic = 4.0 * 0.044715 * linear
    sent_ref[...] = jnp.zeros_like(sent_ref)
    half = 2 * hid
    kinds = w_third_ref.shape[0]
    second_ref[...] = jnp.zeros_like(second_ref)
    third_ref[...] = jnp.zeros_like(third_ref)
    turned_two = (w_second_ref[...].astype(jnp.float32).T * 0.5).astype(jnp.bfloat16)
    turned_three = w_third_ref[...].astype(jnp.float32).T.astype(jnp.bfloat16)
    for part in range(GROUP):
        rows = slice(part * hid, (part + 1) * hid)
        second_ref[rows, rows] = turned_two
        third_ref[rows, part * kinds : (part + 1) * kinds] = turned_three
        first_ref[0:3, rows] = w_first_ref[...].astype(jnp.float32)
        first_ref[3:4, rows] = b_first_ref[...]
        first_ref[4:5, rows] = b_second_ref[...] * 0.5
    coarse_y, coarse_z = CY * lax.axis_size("gy") // SPAN, NZ // SPAN
    cells = cells_ref[...]
    coarse = jnp.concatenate(
        [cells // (coarse_y * coarse_z), cells // coarse_z % coarse_y, cells % coarse_z], 0
    )
    places = coarse.astype(jnp.float32) * SPAN + offsets_ref[...].astype(jnp.float32)
    places = jnp.concatenate([places, jnp.zeros((5, places.shape[1]), jnp.float32)], 0)
    features = features_ref[...].astype(jnp.float32)
    for block in range(blocks):
        here = slice(block * PB, (block + 1) * PB)
        turned = features[:, here].T
        feats_ref[here, :] = jnp.concatenate([turned] * GROUP, 1)
        spots = places[:, here].T
        point_side = (
            first_ref[0:1, :half] * spots[:, 0:1]
            + first_ref[1:2, :half] * spots[:, 1:2]
            + first_ref[2:3, :half] * spots[:, 2:3]
        )
        cosine, sine = jnp.cos(point_side), jnp.sin(point_side)
        for copy in range(width // half):
            cos_p[block, :, copy * half : (copy + 1) * half] = cosine
            sin_p[block, :, copy * half : (copy + 1) * half] = sine
    lane = lax.broadcasted_iota(jnp.int32, (groups, width), 1)
    group = lax.broadcasted_iota(jnp.int32, (groups, width), 0)
    depth = (group + groups * (lane // hid)).astype(jnp.float32)

    @pl.loop(0, blocks * listed)
    def _(slot):
        block = slot // listed
        place = slot % listed

        @pl.when(place < live_ref[block])
        def _():
            owner = owner_ref[block, place]
            tile = local_ref[block, place]
            cell_x = (CX * row_index + tile // CY).astype(jnp.float32)
            cell_y = (CY * owner + tile % CY).astype(jnp.float32)
            cell_side = (
                first_ref[0:1, :] * cell_x
                + first_ref[1:2, :] * cell_y
                + first_ref[2:3, :] * depth
                + first_ref[3:4, :]
            )
            cos_z[...] = jnp.cos(cell_side)
            sin_z[...] = jnp.sin(cell_side)

            @pl.loop(0, groups // ROWS)
            def _(step):
                start = pl.multiple_of(step * ROWS, ROWS)
                sines = sin_z[pl.ds(start, ROWS), :]
                cosines = cos_z[pl.ds(start, ROWS), :]
                rows = []
                for part in range(ROWS):
                    hidden = (
                        sines[part : part + 1] * cos_p[block]
                        - cosines[part : part + 1] * sin_p[block]
                    ).astype(jnp.bfloat16)
                    half_in = (
                        jnp.dot(hidden, second_ref[...], preferred_element_type=jnp.float32)
                        + first_ref[4:5, :]
                    )
                    bent = jnp.tanh(half_in * (linear + cubic * (half_in * half_in)))
                    second = (half_in + half_in * bent).astype(jnp.bfloat16)
                    kernel = jnp.dot(second, third_ref[...], preferred_element_type=jnp.float32)
                    weighed = kernel * feats_ref[pl.ds(block * PB, PB), :]
                    rows.append(jnp.sum(weighed, axis=0, keepdims=True) * scale)
                sent_ref[owner, block, pl.ds(start, ROWS), :] = jnp.concatenate(rows, axis=0)

    cols, rows_c, wide = chunk_ref.shape
    channels = wide // (cols * blocks)
    for dest in range(cols):
        for block in range(blocks):
            item = dest * blocks + block
            for part in range(GROUP):
                flat[
                    part * groups : (part + 1) * groups, item * channels : (item + 1) * channels
                ] = sent_ref[dest, block, :, part * channels : (part + 1) * channels]
    along_z = jnp.dot(
        table_ref[...],
        flat[...],
        precision=lax.Precision.HIGHEST,
        preferred_element_type=jnp.float32,
    )
    items = lax.broadcasted_iota(jnp.int32, (8, wide), 1) // channels
    codes = jnp.full((8, wide), -1.0, jnp.float32)
    for block in range(blocks):
        for place in range(listed):
            owner = owner_ref[block, place]
            tile = local_ref[block, place]
            code = (owner * CX * CY + tile).astype(jnp.float32)
            code = jnp.where(place < live_ref[block], code, -1.0)
            codes = jnp.where(items == owner * blocks + block, code, codes)
    pair = rows_c - 8
    for dest in range(cols):
        chunk_ref[dest, :pair, :] = along_z[dest * pair : (dest + 1) * pair]
        chunk_ref[dest, pair:, :] = codes


def pair_sums(features, offsets, point_cell, tiles, weights, cols_gy, table):
    w_first, b_first, w_second, b_second, w_third = weights
    tile_owner, tile_local, live_count = tiles
    channels, hid = w_third.shape
    blocks = live_count.shape[0]
    smem = pl.BlockSpec(memory_space=pltpu.SMEM)
    vmem = pl.BlockSpec(memory_space=pltpu.VMEM)
    width = GROUP * hid
    return pl.pallas_call(
        pair_kernel,
        out_shape=(
            jax.ShapeDtypeStruct((cols_gy, blocks, NZ // GROUP, GROUP * channels), jnp.float32),
            jax.ShapeDtypeStruct(
                (cols_gy, table.shape[0] // cols_gy + 8, cols_gy * blocks * channels), jnp.float32
            ),
        ),
        in_specs=[smem] * 3 + [vmem] * 9,
        out_specs=(vmem, vmem),
        scratch_shapes=[
            pltpu.VMEM((blocks, PB, width), jnp.float32),
            pltpu.VMEM((blocks, PB, width), jnp.float32),
            pltpu.VMEM((NZ // GROUP, width), jnp.float32),
            pltpu.VMEM((NZ // GROUP, width), jnp.float32),
            pltpu.VMEM((NZ, cols_gy * blocks * channels), jnp.float32),
            pltpu.VMEM((blocks * PB, GROUP * channels), jnp.float32),
            pltpu.VMEM((8, width), jnp.float32),
            pltpu.VMEM((width, width), jnp.bfloat16),
            pltpu.VMEM((width, GROUP * channels), jnp.bfloat16),
        ],
        name="pair_sums",
    )(
        tile_owner,
        tile_local,
        live_count,
        features,
        offsets,
        point_cell[None],
        w_first.T,
        b_first[None],
        w_second,
        b_second[None],
        w_third,
        table,
    )


def tables(cols_x, cols_y, modes):
    size_x, size_y = CX * cols_x, CY * cols_y
    own_p, own_q = modes // cols_x, modes // cols_y
    scale = 1.0 / math.sqrt(size_x * size_y * NZ)

    def frequencies(length):
        order = np.arange(modes)
        return np.where(order < modes // 2, order, length - modes + order)

    def turn(angle):
        cosine, sine = np.cos(angle), np.sin(angle)
        return np.array([[cosine, -sine], [sine, cosine]])

    z_turns = 2 * np.pi * (np.outer(np.arange(modes), np.arange(NZ)) % NZ) / NZ
    z_table = np.stack([np.cos(z_turns), -np.sin(z_turns)], 0) * scale
    z_table = z_table.reshape(2, cols_y, own_q, NZ).transpose(1, 0, 2, 3).reshape(-1, NZ)
    x_turns = 2 * np.pi * (np.outer(frequencies(size_x), np.arange(size_x)) % size_x) / size_x
    forward = turn(-x_turns).reshape(2, 2, modes // 4, 4, cols_x, CX)
    eye = np.eye(own_p)
    forward = np.einsum("srgkdx,pP->pgskdrPx", forward, eye).reshape(modes * 2 * own_p, -1)
    swapped = forward.reshape(-1, 2, 4, forward.shape[1])
    swapped = np.stack([-swapped[:, 1], swapped[:, 0]], 1).reshape(forward.shape)
    backward = turn(x_turns).reshape(2, 2, modes // 4, 4, cols_x, CX)
    backward = np.einsum("srgkdx,pP->dsPxpgrk", backward, eye).reshape(-1, modes * 2 * own_p)
    y_turns = 2 * np.pi * (np.outer(frequencies(size_y), np.arange(size_y)) % size_y) / size_y
    lift = turn(y_turns).reshape(2, 2, cols_x, own_p, cols_y, CY)
    lift = np.einsum("srepdy,xX->dsxyerpX", lift, np.eye(CX))
    lift = lift.reshape(2 * CX * size_y, -1)
    inverse = np.stack([np.cos(z_turns), -np.sin(z_turns)], 0) * scale
    inverse = inverse.reshape(2, cols_y, own_q, NZ)
    joined = np.concatenate([forward, swapped], 0)
    return [np.asarray(t, np.float32) for t in (z_table, joined, backward, lift, inverse)]


def fourier_kernel(
    chunk_ref,
    raw_ref,
    forward_ref,
    backward_ref,
    lift_ref,
    modes_ref,
    coded_ref,
    held_ref,
    back_ref,
    weights,
    pieces,
    places,
    sent_b,
    got_c,
    spectra,
    mixed,
    sent_d,
    got_d,
    sent_e,
    load_sem,
    send_y,
    recv_y,
    send_x,
    recv_x,
):
    best = lax.Precision.HIGHEST
    cols_x, cols_y = lax.axis_size("gx"), lax.axis_size("gy")
    mine_x, mine_y = lax.axis_index("gx"), lax.axis_index("gy")
    load = pltpu.make_async_copy(modes_ref, weights, load_sem)
    load.start()
    barrier = pltpu.get_barrier_semaphore()
    for step in range(1, cols_y):
        pl.semaphore_signal(barrier, inc=1, device_id={"gy": lax.rem(mine_y + step, cols_y)})
    for step in range(1, cols_x):
        pl.semaphore_signal(barrier, inc=1, device_id={"gx": lax.rem(mine_x + step, cols_x)})
    pl.semaphore_wait(barrier, cols_x + cols_y - 2)

    def exchange(axis, source, target, sends, recvs, stage):
        count, mine = (cols_x, mine_x) if axis == "gx" else (cols_y, mine_y)
        moves = []
        for step in range(1, count):
            other = lax.rem(mine + step, count)
            move = pltpu.make_async_remote_copy(
                src_ref=source.at[other],
                dst_ref=target.at[mine],
                send_sem=sends.at[stage, step],
                recv_sem=recvs.at[stage, step],
                device_id={axis: other},
            )
            move.start()
            moves.append(move)
        own = pltpu.make_async_copy(source.at[mine], target.at[mine], sends.at[stage, 0])
        own.start()
        return own, moves

    def arrive(started):
        own, moves = started
        own.wait()
        for move in moves:
            move.wait_recv()

    def depart(started):
        for move in started[1]:
            move.wait_send()

    first = exchange("gy", chunk_ref, coded_ref, send_y, recv_y, 0)
    whole = exchange("gy", raw_ref, held_ref, send_y, recv_y, 1)
    arrive(first)
    rows_c, wide = coded_ref.shape[1], coded_ref.shape[2]
    own_q = (rows_c - 8) // 2
    channels = pieces.shape[1] // own_q
    items = wide // channels
    span = items * cols_y
    for item in range(items):
        lanes = slice(item * channels, (item + 1) * channels)
        places[item * cols_y : (item + 1) * cols_y, :] = coded_ref[:, rows_c - 8, lanes]
        for part in range(2):
            for q in range(own_q):
                row = part * span + item * cols_y
                pieces[row : row + cols_y, q * channels : (q + 1) * channels] = coded_ref[
                    :, part * own_q + q, lanes
                ]
    own_p = sent_b.shape[1] // (2 * CX)
    modes = own_p * cols_x
    size_y = CY * cols_y
    code = places[:, 0:1].astype(jnp.int32)
    owner = code // (CX * CY)
    x_at = (code // CY) % CX
    y_at = owner * CY + code % CY
    shape = (span, modes * 2 * CX)
    lane = lax.broadcasted_iota(jnp.int32, shape, 1)
    p_at = (lane // (2 * CX * own_p)) * own_p + (lane // CX) % own_p
    imag = (lane // (CX * own_p)) % 2
    freq = jnp.where(p_at < modes // 2, p_at, size_y - modes + p_at)
    turns = (freq * y_at).astype(jnp.float32) * (1.0 / size_y)
    angle = (turns - jnp.floor(turns)) * (2.0 * math.pi)
    hit = (lane % CX == x_at) & (code >= 0)
    cosine = jnp.where(hit, jnp.cos(angle), 0.0)
    sine = jnp.where(hit, jnp.sin(angle), 0.0)
    upper = jnp.where(imag == 0, cosine, -sine)
    lower = jnp.where(imag == 0, sine, cosine)
    spread = jnp.concatenate([upper, lower], 0)
    along_y = lax.dot_general(
        spread,
        pieces[...],
        (((0,), (0,)), ((), ())),
        precision=best,
        preferred_element_type=jnp.float32,
    )
    sent_b[...] = along_y.reshape(sent_b.shape)
    second = exchange("gx", sent_b, got_c, send_x, recv_x, 0)
    arrive(second)
    lanes_w = pieces.shape[1]
    spectra[...] = jnp.dot(
        forward_ref[...],
        got_c[...].reshape(-1, lanes_w),
        precision=best,
        preferred_element_type=jnp.float32,
    )
    load.wait()
    half = modes * 2 * own_p
    quad = 8 * channels
    row_of = lax.broadcasted_iota(jnp.int32, (8, quad), 0)
    lane_of = lax.broadcasted_iota(jnp.int32, (8, quad), 1)
    keep = lane_of // (2 * channels) == row_of % 4

    @pl.loop(0, half // 8)
    def _(group):
        p = group // (modes // 4)
        low = (group % (modes // 4)) * 4
        start = pl.multiple_of(group * 8, 8)
        plain = spectra[pl.ds(start, 8), :]
        turned = spectra[pl.ds(pl.multiple_of(half + group * 8, 8), 8), :]
        outs = []
        for q in range(own_q):
            lanes = slice(q * channels, (q + 1) * channels)
            both = jnp.concatenate([plain[:, lanes], turned[:, lanes]], 1)
            both = jnp.where(keep, jnp.concatenate([both] * 4, 1), 0.0)
            high = both.astype(jnp.bfloat16)
            rest = (both - high.astype(jnp.float32)).astype(jnp.bfloat16)
            tile = weights[pl.ds(low, 4), p, q].reshape(quad, channels)
            out = jnp.dot(
                jnp.concatenate([high, rest], 0), tile, preferred_element_type=jnp.float32
            )
            outs.append(out[:8] + out[8:])
        mixed[pl.ds(start, 8), :] = jnp.concatenate(outs, 1)

    along_x = jnp.dot(
        backward_ref[...], mixed[...], precision=best, preferred_element_type=jnp.float32
    )
    sent_d[...] = along_x.reshape(sent_d.shape)
    third = exchange("gx", sent_d, got_d, send_x, recv_x, 1)
    arrive(third)
    along_y = jnp.dot(
        lift_ref[...],
        got_d[...].reshape(-1, lanes_w),
        precision=best,
        preferred_element_type=jnp.float32,
    )
    sent_e[...] = along_y.reshape(sent_e.shape)
    fourth = exchange("gy", sent_e, back_ref, send_y, recv_y, 2)
    arrive(fourth)
    arrive(whole)
    for started in (first, whole, second, third, fourth):
        depart(started)


def fourier(chunk, raw, w_modes, forward, backward, lift):
    cols_x, cols_y = lax.axis_size("gx"), lax.axis_size("gy")
    own_p, own_q = w_modes.shape[1:3]
    modes, channels = w_modes.shape[0], w_modes.shape[-1]
    lanes = own_q * channels
    items = chunk.shape[2] // channels
    vmem = pl.BlockSpec(memory_space=pltpu.VMEM)
    parcel = (cols_x, 2 * own_p * CX, lanes)
    last = (cols_y, 2 * CX * CY, lanes)
    f32 = jnp.float32
    return pl.pallas_call(
        fourier_kernel,
        out_shape=(
            jax.ShapeDtypeStruct(chunk.shape, f32),
            jax.ShapeDtypeStruct(raw.shape, f32),
            jax.ShapeDtypeStruct(last, f32),
        ),
        in_specs=[vmem] * 5 + [pl.BlockSpec(memory_space=pl.ANY)],
        out_specs=(vmem, vmem, vmem),
        scratch_shapes=[
            pltpu.VMEM(w_modes.shape, w_modes.dtype),
            pltpu.VMEM((2 * items * cols_y, lanes), f32),
            pltpu.VMEM((items * cols_y, channels), f32),
            pltpu.VMEM(parcel, f32),
            pltpu.VMEM(parcel, f32),
            pltpu.VMEM((forward.shape[0], lanes), f32),
            pltpu.VMEM((forward.shape[0] // 2, lanes), f32),
            pltpu.VMEM(parcel, f32),
            pltpu.VMEM(parcel, f32),
            pltpu.VMEM(last, f32),
            pltpu.SemaphoreType.DMA,
            pltpu.SemaphoreType.DMA((3, cols_y)),
            pltpu.SemaphoreType.DMA((3, cols_y)),
            pltpu.SemaphoreType.DMA((2, cols_x)),
            pltpu.SemaphoreType.DMA((2, cols_x)),
        ],
        compiler_params=pltpu.CompilerParams(collective_id=0, has_side_effects=True),
        name="fourier",
    )(chunk, raw, forward, backward, lift, w_modes)


def local(
    features,
    offsets,
    point_cell,
    tile_owner,
    tile_local,
    live_count,
    w_first,
    b_first,
    w_second,
    b_second,
    w_third,
    w_point,
    b_point,
    w_modes,
):
    best = lax.Precision.HIGHEST
    rows_gx = lax.axis_size("gx")
    cols_gy = lax.axis_size("gy")
    listed = tile_owner.shape[1]
    channels = w_third.shape[0]
    weights = (w_first, b_first, w_second, b_second, w_third)
    modes = w_modes.shape[0]
    z_table, forward, backward, lift, inverse = tables(rows_gx, cols_gy, modes)
    sums, chunk = pair_sums(
        features,
        offsets,
        point_cell,
        (tile_owner, tile_local, live_count),
        weights,
        cols_gy,
        z_table,
    )
    coded, held, back = fourier(chunk, sums, w_modes, forward, backward, lift)
    blocks_dev = live_count.shape[0]
    codes = coded[:, -8, ::channels].reshape(cols_gy, cols_gy, blocks_dev)
    me = lax.axis_index("gy")
    codes = lax.dynamic_index_in_dim(codes, me, 1, False).reshape(-1)
    received = held.reshape(-1, NZ // GROUP, GROUP, channels).transpose(0, 3, 2, 1)
    received = received.reshape(-1, channels, NZ)
    own_tiles = jnp.arange(CX * CY, dtype=jnp.int32) + me * (CX * CY)
    tile_match = (codes[None, :] == own_tiles[:, None].astype(jnp.float32)).astype(jnp.float32)
    latent = jnp.dot(tile_match, received.reshape(-1, channels * NZ), precision=best)
    latent = latent.reshape(CX, CY, channels, NZ)
    back = back.reshape(cols_gy, 2, CX, CY, -1, channels)
    spectral = jnp.einsum("vsxyqc,svqz->xycz", back, inverse, precision=best)
    pointwise = jnp.einsum("xycz,co->xyoz", latent, w_point.astype(jnp.float32), precision=best)
    return jax.nn.gelu(spectral + pointwise + b_point[:, None])


def solution(mesh):
    placed = (
        P(None, ("gx", "gy")),
        P(None, ("gx", "gy")),
        P(("gx", "gy")),
        P(("gx", "gy"), None),
        P(("gx", "gy"), None),
        P(("gx", "gy")),
        P(),
        P(),
        P(),
        P(),
        P(),
        P(),
        P(),
        P(None, "gx", "gy", None, None, None),
    )
    return jax.shard_map(
        local, mesh=mesh, in_specs=placed, out_specs=P("gx", "gy", None, None), check_vma=False
    )
```

profile of v0, /device:TPU:0, one launch (start us, length us, event | category | flops | bytes accessed | tf_op | source)
XLA Modules:
  0.0 76.1 jit_solution(14605335894581847594)
XLA Ops:
  0.0 0.0 copy-start
  0.0 0.0 copy-start.2
  0.0 0.0 copy-start.1
  0.0 22.1 %pair_sums.1 = (f32[4,2,32,128]{3,2,1,0:T(8,128)}, f32[4,24,256]{2,1,0:T(8,128)}) custom-call(s32[2,4]{1,0:T(2,128)} %owner_ref.1, s32[2,4]{1,0:T(2,128)} %local_ref.1, s32[2]{0:T(128)} %live_ref.1, bf16[32,256]{1,0:T(8,128)(2,1)} %features_ref.1, bf16[3,256]{1,0:T(4,128)(2,1)} %offsets_ref.1, s32[1,256]{1,0:T(1,128)} %bitcast.43, bf16[3,64]{1,0:T(4,128)(2,1)} %bitcast.44, ...), custom_call_target="tpu_custom_call" | custom-call | tf_op jit(solution)/shard_map/pair_sums/pallas_call | solution.py:175
  22.1 46.0 %fourier.1 = (f32[4,24,256]{2,1,0:T(8,128)}, f32[4,2,32,128]{3,2,1,0:T(8,128)}, f32[4,64,256]{2,1,0:T(8,128)}) custom-call(f32[4,24,256]{2,1,0:T(8,128)} %get-tuple-element.10.chunk_ref, f32[4,2,32,128]{3,2,1,0:T(8,128)} %get-tuple-element.11.raw_ref, f32[512,256]{1,0:T(8,128)} %constant.33.clone.forward_ref, f32[256,256]{1,0:T(8,128)} %constant.34.clone.backward_ref, ...), custom_call_target="tpu_custom_call" | custom-call | tf_op jit(solution)/shard_map/fourier/pallas_call | solution.py:425
  68.2 1.2 %reshape.31 = f32[4,2,4,8,8,32]{5,4,3,2,1,0:T(8,128)S(1)} reshape(f32[4,64,256]{2,1,0:T(8,128)} %get-tuple-element.12) | data formatting | bytes 524288 | tf_op jit(solution)/shard_map/reshape | solution.py:500
  69.4 0.0 copy-done.2
  69.4 1.8 %convolution_bitcast_fusion.1 = f32[4,8,32,128]{3,2,1,0:T(8,128)S(1)} fusion(f32[2,4,8,128,1,1]{3,2,5,4,1,0:T(8,128)S(1)} %copy-done.2, f32[4,2,4,8,8,32]{5,4,3,2,1,0:T(8,128)S(1)} %reshape.31), kind=kOutput, calls=%fused_computation.3 | convolution fusion | flops 100663296 | bytes 819200 | tf_op jit(solution)/shard_map/vsxyqc,svqz->xycz/dot_general | solution.py:501
  71.2 1.2 %reshape.32 = f32[8,32,4,32]{3,2,1,0:T(4,128)S(1)} reshape(f32[4,2,32,128]{3,2,1,0:T(8,128)} %get-tuple-element.14) | data formatting | bytes 262144 | tf_op jit(solution)/shard_map/reshape | solution.py:494
  72.4 0.2 copy.27
  72.6 0.4 reshape_reshape.3
  73.1 0.8 %slice.3 = f32[4,1,8]{2,1,0:T(1,128)S(1)} slice(f32[4,24,256]{2,1,0:T(8,128)} %get-tuple-element.13), slice={[0:4:1], [16:17:1], [0:256:32]} | slice | bytes 256 | tf_op jit(solution)/shard_map/slice | solution.py:491
  73.9 0.1 copy.25
  74.0 0.1 copy.26
  74.1 0.1 eq.20
  74.2 0.4 fusion.11
  74.6 0.0 copy-done
  74.6 0.0 copy-done.1
  74.7 1.4 %fusion.9 = f32[4,8,32,128]{3,2,1,0:T(8,128)} fusion(f32[4,8,32,128]{3,2,1,0:T(8,128)S(1)} %convolution_bitcast_fusion.1, f32[4,8,32,128]{3,1,2,0:T(8,128)S(1)} %fusion.11, f32[32]{0:T(128)S(1)} %copy-done.1, bf16[32,32]{1,0:T(8,128)(2,1)S(1)} %copy-done), kind=kOutput, calls=%fused_computation.12 | convolution fusion | flops 51642368 | bytes 1575040 | tf_op jit(solution)/shard_map/xycz,co->xyoz/dot_general | solution.py:502
  (2 shorter events, 0.0 us)
Async XLA Ops:
  0.0 74.6 %copy-start = (bf16[32,32]{1,0:T(8,128)(2,1)S(1)}, bf16[32,32]{1,0:T(8,128)(2,1)}, u32[]{:S(2)}) copy-start(bf16[32,32]{1,0:T(8,128)(2,1)} %param.30) | copy-start | bytes 6148
  0.0 69.4 %copy-start.2 = (f32[2,4,8,128,1,1]{3,2,5,4,1,0:T(8,128)S(1)}, f32[2,4,8,128,1,1]{3,2,5,4,1,0:T(8,128)}, u32[]{:S(2)}) copy-start(f32[2,4,8,128,1,1]{3,2,5,4,1,0:T(8,128)} %constant.41) | copy-start | bytes 98308
  0.0 74.6 %copy-start.1 = (f32[32]{0:T(128)S(1)}, f32[32]{0:T(128)}, u32[]{:S(2)}) copy-start(f32[32]{0:T(128)} %param.31) | copy-start | bytes 388
where the time goes:
time: 76.8 us; the launch traced here: 76.1 us
  Pallas kernels  68.2 us (89%)
  local copies, waits for them, and re-layouts  4.18 us (5%)
  matrix products  3.63 us (5%)
    pallas_call x1, Pallas kernels, fourier(): pl.pallas_call(fourier_kernel, out_shape=(jax.ShapeDtypeStruct(chunk.shap...  46 us
    pallas_call x1, Pallas kernels, pair_sums(): pl.pallas_call(pair_kernel, out_shape=(jax.ShapeDtypeStruct((cols_gy, blo...  22.1 us
    dot_general x1, matrix products, local(): spectral = jnp.einsum('vsxyqc,svqz->xycz', back, inverse, precision=best)  1.79 us

commit v1 on v0

v1 whole, which is shorter than its diff:
```python
import math

import jax
import numpy as np
import jax.numpy as jnp
from jax import lax
from jax.experimental import pallas as pl
from jax.experimental.pallas import tpu as pltpu
from jax.sharding import PartitionSpec as P

NZ = 128
CX = 4
CY = 8
SPAN = 16
PB = 128
LANES = 128

GROUP = 4
UNROLL = 8

LINEAR = 2.0 * math.sqrt(2.0 / math.pi)
CUBIC = 4.0 * 0.044715 * LINEAR

f32 = jnp.float32
bf16 = jnp.bfloat16


def halves(value):
    high = value.astype(bf16)
    return high, (value - high.astype(f32)).astype(bf16)


def split_rows(value):
    high, low = halves(value)
    return jnp.concatenate([high, low, high], 0)


def split_table(table):
    table = np.asarray(table, np.float32)
    high = table.astype(jnp.bfloat16)
    low = (table - high.astype(np.float32)).astype(jnp.bfloat16)
    return np.concatenate([high, high, low], 1)


def matmul(left, right):
    return jnp.dot(left, right, preferred_element_type=f32)


def tables(cols_x, cols_y, modes):
    size_x, size_y = CX * cols_x, CY * cols_y
    own_p, own_q = modes // cols_x, modes // cols_y
    scale = 1.0 / math.sqrt(size_x * size_y * NZ)

    def frequencies(length):
        order = np.arange(modes)
        return np.where(order < modes // 2, order, length - modes + order)

    def turn(angle):
        cosine, sine = np.cos(angle), np.sin(angle)
        return np.array([[cosine, -sine], [sine, cosine]])

    z_turns = 2 * np.pi * (np.outer(np.arange(modes), np.arange(NZ)) % NZ) / NZ
    waves = np.stack([np.cos(z_turns), -np.sin(z_turns)], 0) * scale
    waves = waves.reshape(2, cols_y, own_q, NZ)
    z_table = waves.transpose(2, 0, 1, 3).reshape(-1, NZ)
    inverse = waves.transpose(2, 1, 0, 3).reshape(-1, NZ)
    inverse = np.asarray(inverse, np.float32)
    high = inverse.astype(jnp.bfloat16)
    low = (inverse - high.astype(np.float32)).astype(jnp.bfloat16)
    inverse = np.concatenate([high, high, low], 0)
    x_turns = 2 * np.pi * (np.outer(frequencies(size_x), np.arange(size_x)) % size_x) / size_x
    backward = turn(x_turns).reshape(2, 2, modes // 4, 4, cols_x, CX)
    backward = np.einsum("srgkdx,pP->dsPxpgrk", backward, np.eye(own_p))
    backward = backward.reshape(-1, modes * 2 * own_p)
    y_turns = 2 * np.pi * (np.outer(frequencies(size_y), np.arange(size_y)) % size_y) / size_y
    lift = turn(y_turns).reshape(2, 2, cols_x, own_p, cols_y, CY)
    lift = np.einsum("srepdy,xX->dsxyerpX", lift, np.eye(CX))
    lift = lift.reshape(2 * CX * size_y, -1)
    return split_table(z_table), split_table(backward), split_table(lift), inverse


def encoder_kernel(
    owner_ref,
    local_ref,
    live_ref,
    features_ref,
    offsets_ref,
    cells_ref,
    turned_first_ref,
    b_first_ref,
    w_second_ref,
    b_second_ref,
    w_third_ref,
    z_table_ref,
    backward_ref,
    lift_ref,
    modes_ref,
    codes_ref,
    held_ref,
    back_ref,
    weights,
    cell_sin,
    cell_cos,
    point_sin,
    point_cos,
    spread_two,
    spread_three,
    feats,
    second,
    sums,
    code_sent,
    code_got,
    sent_a,
    got_a,
    raw_sent,
    phases,
    splits,
    spectra,
    mixed,
    sent_d,
    got_d,
    sent_e,
    load_sem,
    sends,
    recvs,
):
    cols_x, cols_y = lax.axis_size("gx"), lax.axis_size("gy")
    mine_x, mine_y = lax.axis_index("gx"), lax.axis_index("gy")
    count = cols_x * cols_y
    me = mine_x * cols_y + mine_y
    blocks, listed = owner_ref.shape
    hid = w_second_ref.shape[0]
    channels = w_third_ref.shape[0]
    wide = GROUP * hid
    two = 2 * hid
    quarter = PB // GROUP
    size_x, size_y = CX * cols_x, CY * cols_y
    load = pltpu.make_async_copy(modes_ref, weights, load_sem)
    load.start()

    def everyone(body):
        if count <= 32:
            for step in range(1, count):
                body(step)
        else:
            pl.loop(1, count)(body)

    def place(step):
        other = lax.rem(me + step, count)
        return other // cols_y, lax.rem(other, cols_y)

    barrier = pltpu.get_barrier_semaphore()

    def greet(step):
        x, y = place(step)
        pl.semaphore_signal(barrier, inc=1, device_id={"gx": x, "gy": y})

    everyone(greet)

    turned_two = (w_second_ref[...].astype(f32).T * 0.5).astype(bf16)
    turned_three = w_third_ref[...].astype(f32).T
    spread_two[...] = jnp.zeros_like(spread_two)
    spread_three[...] = jnp.zeros_like(spread_three)
    for part in range(GROUP):
        rows = slice(part * hid, (part + 1) * hid)
        spread_two[rows, rows] = turned_two
    bias = jnp.concatenate([b_second_ref[...] * 0.5] * GROUP, 1)
    wide_three = jnp.concatenate([turned_three] * GROUP, 1)
    coarse_y, coarse_z = size_y // SPAN, NZ // SPAN
    cells = cells_ref[...]
    coarse = jnp.concatenate(
        [cells // (coarse_y * coarse_z), cells // coarse_z % coarse_y, cells % coarse_z], 0
    )
    places = coarse.astype(f32) * SPAN + offsets_ref[...].astype(f32)
    places = jnp.concatenate([places, jnp.zeros((5, places.shape[1]), f32)], 0)
    turned_first = turned_first_ref[...].astype(f32)
    double_first = jnp.concatenate([turned_first, turned_first], 1)
    features = features_ref[...].astype(f32)

    steps = lax.broadcasted_iota(jnp.int32, (24, two), 0)
    steps = jnp.where(steps < 16, steps * 8, steps - 16).astype(f32)
    steps = steps * double_first[2:3]
    cosine, sine = jnp.cos(steps), jnp.sin(steps)
    cos_fine, sin_fine = cosine[16:24], sine[16:24]
    bases = []
    for block in range(blocks):
        for slot in range(listed):
            tile = local_ref[block, slot]
            cell_x = (CX * mine_x + tile // CY).astype(f32)
            cell_y = (CY * owner_ref[block, slot] + tile % CY).astype(f32)
            bases.append(
                turned_first[0:1] * cell_x + turned_first[1:2] * cell_y + b_first_ref[...]
            )
    base = jnp.concatenate(bases, 0)
    base = jnp.concatenate([base, base], 1)
    base_sin, base_cos = jnp.sin(base), jnp.cos(base)
    code_lane = lax.broadcasted_iota(jnp.int32, (1, LANES), 1)
    code_rows = []
    for block in range(blocks):
        row = jnp.zeros((1, LANES), jnp.int32)
        for slot in range(listed):
            code = owner_ref[block, slot] * (CX * CY) + local_ref[block, slot]
            row = jnp.where(code_lane % listed == slot, code, row)
        code_rows.append(row)
    for block in range(blocks):
        row = jnp.full((1, LANES), -1, jnp.int32)
        for slot in range(listed):
            alive = jnp.where(slot < live_ref[block], local_ref[block, slot], -1)
            row = jnp.where(code_lane == owner_ref[block, slot], alive, row)
        code_rows.append(row)
    code_rows.append(jnp.zeros((8 - 2 * blocks, LANES), jnp.int32))
    code_sent[...] = jnp.concatenate(code_rows, 0)

    lane = lax.broadcasted_iota(jnp.int32, (quarter, two), 1)

    def pairs(block):
        here = slice(block * PB, (block + 1) * PB)
        for slot in range(listed):
            item = block * listed + slot
            b_sin, b_cos = base_sin[item : item + 1], base_cos[item : item + 1]
            near_sin = sin_fine * b_cos + cos_fine * b_sin
            near_cos = cos_fine * b_cos - sin_fine * b_sin
            for step in range(NZ // 8):
                rows = slice(slot * NZ + step * 8, slot * NZ + step * 8 + 8)
                far_cos, far_sin = cosine[step : step + 1], sine[step : step + 1]
                cell_sin[rows, :] = far_cos * near_sin + far_sin * near_cos
                cell_cos[rows, :] = far_cos * near_cos - far_sin * near_sin
        spots = places[:, here].T
        side = (
            double_first[0:1] * spots[:, 0:1]
            + double_first[1:2] * spots[:, 1:2]
            + double_first[2:3] * spots[:, 2:3]
        )
        side_cos, side_sin = jnp.cos(side), jnp.sin(side)
        for half in range(GROUP // 2):
            low = slice(2 * half * quarter, (2 * half + 1) * quarter)
            up = slice((2 * half + 1) * quarter, (2 * half + 2) * quarter)
            cols = slice(half * two, (half + 1) * two)
            point_cos[:, cols] = jnp.where(lane < hid, side_cos[low], side_cos[up])
            point_sin[:, cols] = jnp.where(lane < hid, side_sin[low], side_sin[up])
        turned = features[:, here].T
        feats[...] = jnp.concatenate(
            [turned[j * quarter : (j + 1) * quarter] for j in range(GROUP)], 1
        )
        sums[...] = jnp.zeros_like(sums)

        @pl.loop(0, quarter // UNROLL)
        def _(step):
            for inner in range(UNROLL):
                weigh = wide_three * feats[pl.ds(step * UNROLL + inner, 1), :]
                high, rest = halves(weigh)
                for part in range(GROUP):
                    rows = slice(inner * wide + part * hid, inner * wide + (part + 1) * hid)
                    cols = slice(part * channels, (part + 1) * channels)
                    spread_three[rows, part * channels : (part + 1) * channels] = high[:, cols]
                    spread_three[
                        rows, LANES + part * channels : LANES + (part + 1) * channels
                    ] = rest[:, cols]
            for slot in range(listed):
                rows = slice(slot * NZ, (slot + 1) * NZ)
                for inner in range(UNROLL):
                    group = step * UNROLL + inner
                    p_cos, p_sin = point_cos[pl.ds(group, 1), :], point_sin[pl.ds(group, 1), :]
                    c_sin, c_cos = cell_sin[rows, :], cell_cos[rows, :]
                    hidden = []
                    for half in range(GROUP // 2):
                        cols = slice(half * two, (half + 1) * two)
                        value = c_sin * p_cos[:, cols] - c_cos * p_sin[:, cols]
                        hidden.append(value.astype(bf16))
                    y = matmul(jnp.concatenate(hidden, 1), spread_two[...]) + bias
                    bent = jnp.tanh(y * (LINEAR + CUBIC * (y * y)))
                    second[rows, inner * wide : (inner + 1) * wide] = (y + y * bent).astype(bf16)
                sums[rows, :] += matmul(second[rows, :], spread_three[...])

    own_q = sent_a.shape[3] // channels
    lane_z = lax.broadcasted_iota(jnp.int32, (NZ, LANES), 1) // channels
    lane_r = lax.broadcasted_iota(jnp.int32, (quarter, LANES), 1) // channels
    scale = 1.0 / math.sqrt(PB)

    def parcels(block):
        flat = jnp.zeros((NZ, LANES), f32)
        dense = []
        for slot in range(listed):
            rows = slice(slot * NZ, (slot + 1) * NZ)
            total = sums[rows, 0:LANES] + sums[rows, LANES:]
            total = total + pltpu.roll(total, 2 * channels, 1)
            total = total + pltpu.roll(total, channels, 1)
            total = jnp.where(slot < live_ref[block], total * scale, 0.0)
            flat = jnp.where(lane_z == slot, total, flat)
            tight = total[0:quarter]
            for part in range(1, GROUP):
                tight = jnp.where(
                    lane_r == part, total[part * quarter : (part + 1) * quarter], tight
                )
            dense.append(tight)
        modes = matmul(z_table_ref[...], split_rows(flat))
        span = 2 * cols_y
        for slot in range(listed):
            lanes = slice(slot * channels, (slot + 1) * channels)
            joined = jnp.concatenate(
                [modes[q * span : (q + 1) * span, lanes] for q in range(own_q)], 1
            )
            for part in range(2):
                sent_a[block, :, part * listed + slot, :] = joined[
                    part * cols_y : (part + 1) * cols_y
                ]
        for dest in range(cols_y):
            chosen = jnp.zeros((quarter, LANES), f32)
            for slot in range(listed):
                chosen = jnp.where(owner_ref[block, slot] == dest, dense[slot], chosen)
            raw_sent[dest, block] = chosen

    def send(source, target, stage, x, y):
        pltpu.make_async_remote_copy(
            src_ref=source,
            dst_ref=target,
            send_sem=sends.at[stage],
            recv_sem=recvs.at[stage],
            device_id={"gx": x, "gy": y},
        ).start()

    def keep(source, target, stage):
        pltpu.make_async_copy(source, target, recvs.at[stage]).start()

    def spread(block):
        def go(step):
            x, y = place(step)
            send(sent_a.at[block, y], got_a.at[block, me], block, x, y)

        everyone(go)
        keep(sent_a.at[block, mine_y], got_a.at[block, me], block)

    def arrive(target, stage):
        pltpu.make_async_copy(target, target, recvs.at[stage]).wait()

    def depart(part, stage):
        pltpu.make_async_copy(part, part, sends.at[stage]).wait()

    stage_code, stage_raw, stage_d, stage_e = blocks, blocks + 1, blocks + 2, blocks + 3

    pairs(0)
    parcels(0)
    pl.semaphore_wait(barrier, count - 1)

    def tell(step):
        x, y = place(step)
        send(code_sent, code_got.at[me], stage_code, x, y)

    everyone(tell)
    keep(code_sent, code_got.at[me], stage_code)
    spread(0)
    for block in range(1, blocks):
        pairs(block)
        parcels(block)
        spread(block)

    for step in range(1, cols_y):
        other = lax.rem(mine_y + step, cols_y)
        send(raw_sent.at[other], held_ref.at[mine_y], stage_raw, mine_x, other)
    keep(raw_sent.at[mine_y], held_ref.at[mine_y], stage_raw)

    arrive(code_got, stage_code)
    own_p = sent_d.shape[1] // (2 * CX)
    modes = own_p * cols_x
    each = 2 * listed
    depth = count * each
    column = lax.broadcasted_iota(jnp.int32, (1, depth), 1)
    source = column // each
    slots = modes * 2
    row = lax.broadcasted_iota(jnp.int32, (slots, depth), 0)
    which = (row // 8) * 4 + row % 4
    freq_x = jnp.where(which < modes // 2, which, size_x - modes + which)
    part_out = (row // 4) % 2
    part_in = (column // listed) % 2
    quarters = (part_out - part_in).astype(f32) * 0.25
    p_at = mine_x * own_p + lax.broadcasted_iota(jnp.int32, (own_p, depth), 0)
    freq_y = jnp.where(p_at < modes // 2, p_at, size_y - modes + p_at)
    owns = (
        lax.broadcasted_iota(jnp.int32, (count, depth), 1) // each
        == lax.broadcasted_iota(jnp.int32, (count, depth), 0)
    )

    def waves(turns):
        angle = (turns - jnp.floor(turns)) * (2.0 * math.pi)
        return jnp.cos(angle), jnp.sin(angle)

    for block in range(blocks):
        codes = jnp.concatenate([code_got[:, block, :].astype(f32)] * (depth // LANES), 1)
        code = jnp.sum(jnp.where(owns, codes, 0.0), axis=0, keepdims=True).astype(jnp.int32)
        tile = code % (CX * CY)
        x_at = CX * (source // cols_y) + tile // CY
        y_at = CY * (code // (CX * CY)) + tile % CY
        x_cos, x_sin = waves((freq_x * x_at).astype(f32) * (1.0 / size_x) + quarters)
        y_cos, y_sin = waves((freq_y * y_at).astype(f32) * (1.0 / size_y))
        for p in range(own_p):
            value = x_cos * y_cos[p : p + 1] - x_sin * y_sin[p : p + 1]
            high, low = halves(value)
            rows = slice(p * slots, (p + 1) * slots)
            start = block * 3 * depth
            phases[rows, start : start + depth] = high
            phases[rows, start + depth : start + 2 * depth] = high
            phases[rows, start + 2 * depth : start + 3 * depth] = low
    lanes_w = got_a.shape[3]
    for block in range(blocks):
        arrive(got_a.at[block], block)
        splits[block * 3 * depth : (block + 1) * 3 * depth, :] = split_rows(
            got_a[block].reshape(depth, lanes_w)
        )
    spectra[...] = matmul(phases[...], splits[...])

    load.wait()
    quad = 8 * channels
    row_of = lax.broadcasted_iota(jnp.int32, (8, quad), 0)
    lane_of = lax.broadcasted_iota(jnp.int32, (8, quad), 1)
    own_four = lane_of // (2 * channels) == row_of % 4
    negate = lax.broadcasted_iota(jnp.int32, (8, lanes_w), 0) < 4
    fours = modes // 4
    ahead = 4

    @pl.loop(0, own_p * fours // ahead)
    def _(outer):
        for inner in range(ahead):
            group = outer * ahead + inner
            p = group // fours
            low = (group % fours) * 4
            start = pl.multiple_of(group * 8, 8)
            plain = spectra[pl.ds(start, 8), :]
            turned = pltpu.roll(plain, 4, 0)
            turned = jnp.where(negate, -turned, turned)
            outs = []
            for q in range(own_q):
                lanes = slice(q * channels, (q + 1) * channels)
                both = jnp.concatenate([plain[:, lanes], turned[:, lanes]], 1)
                both = jnp.where(own_four, jnp.concatenate([both] * 4, 1), 0.0)
                high, rest = halves(both)
                tile = weights[pl.ds(low, 4), p, q].reshape(quad, channels)
                out = matmul(jnp.concatenate([high, rest], 0), tile)
                outs.append(out[:8] + out[8:])
            mixed[pl.ds(start, 8), :] = jnp.concatenate(outs, 1)

    along_x = matmul(backward_ref[...], split_rows(mixed[...]))
    sent_d[...] = along_x.reshape(sent_d.shape)
    for step in range(1, cols_x):
        other = lax.rem(mine_x + step, cols_x)
        send(sent_d.at[other], got_d.at[mine_x], stage_d, other, mine_y)
    keep(sent_d.at[mine_x], got_d.at[mine_x], stage_d)
    arrive(got_d, stage_d)
    along_y = matmul(lift_ref[...], split_rows(got_d[...].reshape(-1, lanes_w)))
    sent_e[...] = along_y.reshape(sent_e.shape)
    for step in range(1, cols_y):
        other = lax.rem(mine_y + step, cols_y)
        send(sent_e.at[other], back_ref.at[mine_y], stage_e, mine_x, other)
    keep(sent_e.at[mine_y], back_ref.at[mine_y], stage_e)
    codes_ref[...] = code_got[pl.ds(mine_x * cols_y, cols_y)]
    for block in range(blocks):
        depart(got_a.at[block, pl.ds(0, count - 1)], block)
    depart(code_got.at[pl.ds(0, count - 1)], stage_code)
    depart(raw_sent.at[pl.ds(0, cols_y - 1)], stage_raw)
    depart(sent_d.at[pl.ds(0, cols_x - 1)], stage_d)
    arrive(held_ref, stage_raw)
    arrive(back_ref, stage_e)
    depart(sent_e.at[pl.ds(0, cols_y - 1)], stage_e)


def encoder(
    features,
    offsets,
    point_cell,
    tile_owner,
    tile_local,
    live_count,
    w_first,
    b_first,
    w_second,
    b_second,
    w_third,
    w_modes,
    z_table,
    backward,
    lift,
):
    cols_x, cols_y = lax.axis_size("gx"), lax.axis_size("gy")
    count = cols_x * cols_y
    own_p, own_q = w_modes.shape[1:3]
    modes, channels = w_modes.shape[0], w_modes.shape[-1]
    hid = w_third.shape[1]
    blocks, listed = tile_owner.shape
    lanes = own_q * channels
    wide = GROUP * hid
    quarter = PB // GROUP
    depth = count * 2 * listed
    slots = modes * 2 * own_p
    smem = pl.BlockSpec(memory_space=pltpu.SMEM)
    vmem = pl.BlockSpec(memory_space=pltpu.VMEM)
    last = (cols_y, 2 * CX * CY, lanes)
    parcel = (cols_x, 2 * own_p * CX, lanes)
    return pl.pallas_call(
        encoder_kernel,
        out_shape=(
            jax.ShapeDtypeStruct((cols_y, 8, LANES), jnp.int32),
            jax.ShapeDtypeStruct((cols_y, blocks, quarter, LANES), f32),
            jax.ShapeDtypeStruct(last, f32),
        ),
        in_specs=[smem] * 3 + [vmem] * 11 + [pl.BlockSpec(memory_space=pl.ANY)],
        out_specs=(vmem, vmem, vmem),
        scratch_shapes=[
            pltpu.VMEM(w_modes.shape, w_modes.dtype),
            pltpu.VMEM((listed * NZ, 2 * hid), f32),
            pltpu.VMEM((listed * NZ, 2 * hid), f32),
            pltpu.VMEM((quarter, wide), f32),
            pltpu.VMEM((quarter, wide), f32),
            pltpu.VMEM((wide, wide), bf16),
            pltpu.VMEM((UNROLL * wide, 2 * GROUP * channels), bf16),
            pltpu.VMEM((quarter, GROUP * channels), f32),
            pltpu.VMEM((listed * NZ, UNROLL * wide), bf16),
            pltpu.VMEM((listed * NZ, 2 * GROUP * channels), f32),
            pltpu.VMEM((8, LANES), jnp.int32),
            pltpu.VMEM((count, 8, LANES), jnp.int32),
            pltpu.VMEM((blocks, cols_y, 2 * listed, lanes), f32),
            pltpu.VMEM((blocks, count, 2 * listed, lanes), f32),
            pltpu.VMEM((cols_y, blocks, quarter, LANES), f32),
            pltpu.VMEM((slots, blocks * 3 * depth), bf16),
            pltpu.VMEM((blocks * 3 * depth, lanes), bf16),
            pltpu.VMEM((slots, lanes), f32),
            pltpu.VMEM((slots, lanes), f32),
            pltpu.VMEM(parcel, f32),
            pltpu.VMEM(parcel, f32),
            pltpu.VMEM(last, f32),
            pltpu.SemaphoreType.DMA,
            pltpu.SemaphoreType.DMA((blocks + 4,)),
            pltpu.SemaphoreType.DMA((blocks + 4,)),
        ],
        compiler_params=pltpu.CompilerParams(collective_id=0, has_side_effects=True),
        name="encoder",
    )(
        tile_owner,
        tile_local,
        live_count,
        features,
        offsets,
        point_cell[None],
        w_first.T,
        b_first[None],
        w_second,
        b_second[None],
        w_third,
        z_table,
        backward,
        lift,
        w_modes,
    )


def decoder_kernel(
    codes_ref,
    held_ref,
    back_ref,
    inverse_ref,
    w_point_ref,
    b_point_ref,
    out_ref,
    rolled,
    before,
):
    cols_y, blocks, quarter = held_ref.shape[:3]
    channels = w_point_ref.shape[0]
    mine_y = lax.axis_index("gy")
    groups = LANES // channels
    lanes_w = back_ref.shape[2]
    own_q = lanes_w // channels
    value = back_ref[...].reshape(cols_y * 2 * CX * CY, lanes_w)
    if lanes_w < LANES:
        value = jnp.concatenate([value] * (LANES // lanes_w), 1)
    lane_tiles = value.shape[1] // LANES
    for lane_tile in range(lane_tiles):
        part = value[:, lane_tile * LANES : (lane_tile + 1) * LANES]
        for shift in range(groups):
            rolled[lane_tile, shift] = (
                pltpu.roll(part, shift * channels, 1) if shift else part
            )
    spans = 2 * cols_y
    lane = lax.broadcasted_iota(jnp.int32, (spans, LANES), 1) // channels
    bias = b_point_ref[...]
    for chunk in range(CX * CY // groups):
        rows = []
        for q in range(own_q):
            found = jnp.zeros((spans, LANES), f32)
            for j in range(groups):
                piece = rolled[
                    q // groups,
                    (j - q) % groups,
                    pl.ds(chunk * groups + j, spans, stride=CX * CY),
                    :,
                ]
                found = jnp.where(lane == j, piece, found)
            rows.append(found)
        table = jnp.concatenate(rows, 0)
        high, low = halves(table)
        spectral = lax.dot_general(
            jnp.concatenate([high, low, high], 0),
            inverse_ref[...],
            (((0,), (0,)), ((), ())),
            preferred_element_type=f32,
        )
        for j in range(groups):
            before[chunk * groups + j] = spectral[j * channels : (j + 1) * channels] + bias
    turned = w_point_ref[...].astype(f32).T.astype(bf16)
    turned = jnp.concatenate([turned, turned], 1)
    for source in range(cols_y):
        for block in range(blocks):
            tile = codes_ref[source, blocks + block, mine_y]

            @pl.when(tile >= 0)
            def _():
                flipped = held_ref[source, block].T
                item = jnp.concatenate(
                    [flipped[j * channels : (j + 1) * channels] for j in range(groups)], 1
                )
                high, low = halves(item)
                before[tile] += matmul(turned, jnp.concatenate([high, low], 0))

    root = math.sqrt(2.0 / math.pi)
    for tile in range(CX * CY):
        x = before[tile]
        half = 0.5 * x
        bent = jnp.tanh(x * (root + (0.044715 * root) * (x * x)))
        out_ref[tile // CY, tile % CY] = half + half * bent


def decoder(codes, held, back, inverse, w_point, b_point):
    smem = pl.BlockSpec(memory_space=pltpu.SMEM)
    vmem = pl.BlockSpec(memory_space=pltpu.VMEM)
    channels = w_point.shape[0]
    lane_tiles = max(1, back.shape[2] // LANES)
    rows = back.shape[0] * back.shape[1]
    return pl.pallas_call(
        decoder_kernel,
        out_shape=jax.ShapeDtypeStruct((CX, CY, channels, NZ), f32),
        in_specs=[smem] + [vmem] * 5,
        out_specs=vmem,
        scratch_shapes=[
            pltpu.VMEM((lane_tiles, LANES // channels, rows, LANES), f32),
            pltpu.VMEM((CX * CY, channels, NZ), f32),
        ],
        name="decoder",
    )(codes, held, back, inverse, w_point, b_point[:, None])


def local(
    features,
    offsets,
    point_cell,
    tile_owner,
    tile_local,
    live_count,
    w_first,
    b_first,
    w_second,
    b_second,
    w_third,
    w_point,
    b_point,
    w_modes,
):
    z_table, backward, lift, inverse = tables(
        lax.axis_size("gx"), lax.axis_size("gy"), w_modes.shape[0]
    )
    codes, held, back = encoder(
        features,
        offsets,
        point_cell,
        tile_owner,
        tile_local,
        live_count,
        w_first,
        b_first,
        w_second,
        b_second,
        w_third,
        w_modes,
        z_table,
        backward,
        lift,
    )
    return decoder(codes, held, back, inverse, w_point, b_point)


def solution(mesh):
    placed = (
        P(None, ("gx", "gy")),
        P(None, ("gx", "gy")),
        P(("gx", "gy")),
        P(("gx", "gy"), None),
        P(("gx", "gy"), None),
        P(("gx", "gy")),
        P(),
        P(),
        P(),
        P(),
        P(),
        P(),
        P(),
        P(None, "gx", "gy", None, None, None),
    )
    return jax.shard_map(
        local, mesh=mesh, in_specs=placed, out_specs=P("gx", "gy", None, None), check_vma=False
    )
```

time: 76.8 us -> 54.7 us (0.71)
  Pallas kernels: 68.2 us -> 52.6 us
  matrix products: 3.63 us -> 0 us
  local copies, waits for them, and re-layouts: 4.18 us -> 1.34 us
    pallas_call x2, Pallas kernels: 68.2 us -> 52.6 us  [the longest x1 48.1 us: encoder(): pl.pallas_call(encoder_kernel, out_shape=(jax.ShapeDtypeStruct((cols_y, 8...]
    dot_general x3 -> x0, matrix products: 3.63 us -> none  [the longest x1 1.79 us: local(): spectral = jnp.einsum('vsxyqc,svqz->xycz', back, inverse, precision=best)]
    reshape x3 -> x0, local copies, waits for them, and re-layouts: 2.62 us -> none  [the longest x2 1.4 us: local(): held.reshape(-1, NZ // GROUP, GROUP, channels).transpose(0, 3, 2, 1)]
    broadcast_in_dim x0 -> x1, local copies, waits for them, and re-layouts: none -> 1.34 us  [decoder(): b_point[:, None]]
    slice x2 -> x0, local copies, waits for them, and re-layouts: 0.93 us -> none  [local(): codes = coded[:, -8, ::channels].reshape(cols_gy, cols_gy, blocks_dev)]
where the time goes in v1:
time: 54.7 us; the launch traced here: 54 us
  Pallas kernels  52.6 us (96%)
  local copies, waits for them, and re-layouts  1.34 us (2%)
    pallas_call x1, Pallas kernels, encoder(): pl.pallas_call(encoder_kernel, out_shape=(jax.ShapeDtypeStruct((cols_y, 8...  48.1 us
    pallas_call x1, Pallas kernels, decoder(): pl.pallas_call(decoder_kernel, out_shape=jax.ShapeDtypeStruct((CX, CY, ch...  4.53 us
    broadcast_in_dim x1, local copies, waits for them, and re-layouts, decoder(): b_point[:, None]  1.34 us

profile of v1, /device:TPU:0, one launch (start us, length us, event | category | flops | bytes accessed | tf_op | source)
XLA Modules:
  0.0 54.0 jit_solution(14725442746945726547)
XLA Ops:
  0.0 1.3 %copy.19.b_point_ref = f32[32,1]{1,0:T(8,128)} copy(f32[32,1]{0,1:T(1,128)} %bitcast.9) | data formatting | bytes 256 | tf_op jit(solution)/shard_map/broadcast_in_dim | solution.py:646
  1.3 48.1 %encoder.1 = (s32[4,8,128]{2,1,0:T(8,128)}, f32[4,2,32,128]{3,2,1,0:T(8,128)}, f32[4,64,256]{2,1,0:T(8,128)}) custom-call(s32[2,4]{1,0:T(2,128)} %owner_ref.1, s32[2,4]{1,0:T(2,128)} %local_ref.1, s32[2]{0:T(128)} %live_ref.1, bf16[32,256]{1,0:T(8,128)(2,1)} %features_ref.1, bf16[3,256]{1,0:T(4,128)(2,1)} %offsets_ref.1, s32[1,256]{1,0:T(1,128)} %bitcast.5, ...), custom_call_target="tpu_custom_call" | custom-call | tf_op jit(solution)/shard_map/encoder/pallas_call | solution.py:497
  49.4 4.5 %decoder.1 = f32[4,8,32,128]{3,2,1,0:T(8,128)} custom-call(s32[4,8,128]{2,1,0:T(8,128)} %get-tuple-element.8.codes_ref, f32[4,2,32,128]{3,2,1,0:T(8,128)} %get-tuple-element.9.held_ref, f32[4,64,256]{2,1,0:T(8,128)} %get-tuple-element.10.back_ref, bf16[192,128]{1,0:T(8,128)(2,1)} %constant.11.clone.inverse_ref, bf16[32,32]{1,0:T(8,128)(2,1)} %w_point_ref.1, ...), custom_call_target="tpu_custom_call" | custom-call | tf_op jit(solution)/shard_map/decoder/pallas_call | solution.py:636

commit v2 on v1

--- a/solution.py
+++ b/solution.py
@@ -336,7 +336,8 @@
     def depart(part, stage):
         pltpu.make_async_copy(part, part, sends.at[stage]).wait()
 
-    stage_code, stage_raw, stage_d, stage_e = blocks, blocks + 1, blocks + 2, blocks + 3
+    stage_code, stage_raw, stage_d = blocks, blocks + 1, blocks + 2
+    stage_e = stage_d + sent_d.shape[0]
 
     pairs(0)
     parcels(0)
@@ -360,7 +361,7 @@
     keep(raw_sent.at[mine_y], held_ref.at[mine_y], stage_raw)
 
     arrive(code_got, stage_code)
-    own_p = sent_d.shape[1] // (2 * CX)
+    own_p = sent_d.shape[2] // (2 * CX)
     modes = own_p * cols_x
     each = 2 * listed
     depth = count * each
@@ -409,57 +410,87 @@
     spectra[...] = matmul(phases[...], splits[...])
 
     load.wait()
+    pieces, width = sent_d.shape[0], sent_d.shape[3]
     quad = 8 * channels
-    row_of = lax.broadcasted_iota(jnp.int32, (8, quad), 0)
-    lane_of = lax.broadcasted_iota(jnp.int32, (8, quad), 1)
-    own_four = lane_of // (2 * channels) == row_of % 4
-    negate = lax.broadcasted_iota(jnp.int32, (8, lanes_w), 0) < 4
+    bands = LANES // channels
+    row_of = lax.broadcasted_iota(jnp.int32, (8, LANES), 0)
+    lane_of = lax.broadcasted_iota(jnp.int32, (8, LANES), 1)
+    band = lane_of // channels
+    own_four = [row_of % 4 == 2 * side + lane_of // (2 * channels) for side in range(2)]
+    negate = row_of < 4
     fours = modes // 4
-    ahead = 4
-
-    @pl.loop(0, own_p * fours // ahead)
-    def _(outer):
-        for inner in range(ahead):
-            group = outer * ahead + inner
-            p = group // fours
-            low = (group % fours) * 4
-            start = pl.multiple_of(group * 8, 8)
-            plain = spectra[pl.ds(start, 8), :]
-            turned = pltpu.roll(plain, 4, 0)
-            turned = jnp.where(negate, -turned, turned)
-            outs = []
-            for q in range(own_q):
-                lanes = slice(q * channels, (q + 1) * channels)
-                both = jnp.concatenate([plain[:, lanes], turned[:, lanes]], 1)
-                both = jnp.where(own_four, jnp.concatenate([both] * 4, 1), 0.0)
-                high, rest = halves(both)
-                tile = weights[pl.ds(low, 4), p, q].reshape(quad, channels)
-                out = matmul(jnp.concatenate([high, rest], 0), tile)
-                outs.append(out[:8] + out[8:])
-            mixed[pl.ds(start, 8), :] = jnp.concatenate(outs, 1)
-
-    along_x = matmul(backward_ref[...], split_rows(mixed[...]))
-    sent_d[...] = along_x.reshape(sent_d.shape)
-    for step in range(1, cols_x):
-        other = lax.rem(mine_x + step, cols_x)
-        send(sent_d.at[other], got_d.at[mine_x], stage_d, other, mine_y)
-    keep(sent_d.at[mine_x], got_d.at[mine_x], stage_d)
-    arrive(got_d, stage_d)
-    along_y = matmul(lift_ref[...], split_rows(got_d[...].reshape(-1, lanes_w)))
-    sent_e[...] = along_y.reshape(sent_e.shape)
-    for step in range(1, cols_y):
-        other = lax.rem(mine_y + step, cols_y)
-        send(sent_e.at[other], back_ref.at[mine_y], stage_e, mine_x, other)
-    keep(sent_e.at[mine_y], back_ref.at[mine_y], stage_e)
+    ahead = 8
+
+    for piece in range(pieces):
+        first_q = piece * (width // channels)
+
+        @pl.loop(0, own_p * fours // ahead)
+        def _(outer):
+            for inner in range(ahead):
+                group = outer * ahead + inner
+                p = group // fours
+                low = (group % fours) * 4
+                start = pl.multiple_of(group * 8, 8)
+                plain = spectra[pl.ds(start, 8), piece * width : (piece + 1) * width]
+                plain = jnp.concatenate([plain] * (LANES // width), 1)
+                turned = pltpu.roll(plain, 4, 0)
+                turned = jnp.where(negate, -turned, turned)
+                plains = [plain] + [pltpu.roll(plain, r * channels, 1) for r in range(1, bands)]
+                turns = [turned] + [pltpu.roll(turned, r * channels, 1) for r in range(1, bands)]
+                outs = []
+                for q in range(width // channels):
+                    both = plains[-q % bands]
+                    for at in range(1, bands):
+                        kind = turns if at % 2 else plains
+                        both = jnp.where(band == at, kind[(at - q) % bands], both)
+                    both = jnp.concatenate([jnp.where(own, both, 0.0) for own in own_four], 1)
+                    high, rest = halves(both)
+                    tile = weights[pl.ds(low, 4), p, first_q + q].reshape(quad, channels)
+                    out = matmul(jnp.concatenate([high, rest], 0), tile)
+                    outs.append(out[:8] + out[8:])
+                mixed[pl.ds(start, 8), piece * width : (piece + 1) * width] = jnp.concatenate(
+                    outs, 1
+                )
+
+        along_x = matmul(
+            backward_ref[...], split_rows(mixed[:, piece * width : (piece + 1) * width])
+        )
+        sent_d[piece] = along_x.reshape(sent_d.shape[1:])
+        for step in range(1, cols_x):
+            other = lax.rem(mine_x + step, cols_x)
+            send(
+                sent_d.at[piece, other],
+                got_d.at[piece, mine_x],
+                stage_d + piece,
+                other,
+                mine_y,
+            )
+        keep(sent_d.at[piece, mine_x], got_d.at[piece, mine_x], stage_d + piece)
+    for piece in range(pieces):
+        arrive(got_d.at[piece], stage_d + piece)
+        along_y = matmul(lift_ref[...], split_rows(got_d[piece].reshape(-1, width)))
+        sent_e[piece] = along_y.reshape(sent_e.shape[1:])
+        for step in range(1, cols_y):
+            other = lax.rem(mine_y + step, cols_y)
+            send(
+                sent_e.at[piece, other],
+                back_ref.at[piece, mine_y],
+                stage_e + piece,
+                mine_x,
+                other,
+            )
+        keep(sent_e.at[piece, mine_y], back_ref.at[piece, mine_y], stage_e + piece)
     codes_ref[...] = code_got[pl.ds(mine_x * cols_y, cols_y)]
     for block in range(blocks):
         depart(got_a.at[block, pl.ds(0, count - 1)], block)
     depart(code_got.at[pl.ds(0, count - 1)], stage_code)
     depart(raw_sent.at[pl.ds(0, cols_y - 1)], stage_raw)
-    depart(sent_d.at[pl.ds(0, cols_x - 1)], stage_d)
+    for piece in range(pieces):
+        depart(sent_d.at[piece, pl.ds(0, cols_x - 1)], stage_d + piece)
     arrive(held_ref, stage_raw)
-    arrive(back_ref, stage_e)
-    depart(sent_e.at[pl.ds(0, cols_y - 1)], stage_e)
+    for piece in range(pieces):
+        arrive(back_ref.at[piece], stage_e + piece)
+        depart(sent_e.at[piece, pl.ds(0, cols_y - 1)], stage_e + piece)
 
 
 def encoder(
@@ -492,8 +523,11 @@
     slots = modes * 2 * own_p
     smem = pl.BlockSpec(memory_space=pltpu.SMEM)
     vmem = pl.BlockSpec(memory_space=pltpu.VMEM)
-    last = (cols_y, 2 * CX * CY, lanes)
-    parcel = (cols_x, 2 * own_p * CX, lanes)
+    pieces = max(1, lanes // LANES)
+    width = lanes // pieces
+    last = (pieces, cols_y, 2 * CX * CY, width)
+    parcel = (pieces, cols_x, 2 * own_p * CX, width)
+    stages = blocks + 2 + 2 * pieces
     return pl.pallas_call(
         encoder_kernel,
         out_shape=(
@@ -527,8 +561,8 @@
             pltpu.VMEM(parcel, f32),
             pltpu.VMEM(last, f32),
             pltpu.SemaphoreType.DMA,
-            pltpu.SemaphoreType.DMA((blocks + 4,)),
-            pltpu.SemaphoreType.DMA((blocks + 4,)),
+            pltpu.SemaphoreType.DMA((stages,)),
+            pltpu.SemaphoreType.DMA((stages,)),
         ],
         compiler_params=pltpu.CompilerParams(collective_id=0, has_side_effects=True),
         name="encoder",
@@ -561,89 +595,100 @@
     out_ref,
     rolled,
     before,
+    done,
+    out_sem,
 ):
     cols_y, blocks, quarter = held_ref.shape[:3]
     channels = w_point_ref.shape[0]
     mine_y = lax.axis_index("gy")
     groups = LANES // channels
-    lanes_w = back_ref.shape[2]
-    own_q = lanes_w // channels
-    value = back_ref[...].reshape(cols_y * 2 * CX * CY, lanes_w)
-    if lanes_w < LANES:
-        value = jnp.concatenate([value] * (LANES // lanes_w), 1)
-    lane_tiles = value.shape[1] // LANES
-    for lane_tile in range(lane_tiles):
-        part = value[:, lane_tile * LANES : (lane_tile + 1) * LANES]
+    pieces, width = back_ref.shape[0], back_ref.shape[3]
+    each = width // channels
+    bias = jnp.concatenate([b_point_ref[...]] * channels, 0).T[:, 0:1]
+    before[...] = jnp.zeros_like(before)
+    turned = w_point_ref[...].astype(f32).T.astype(bf16)
+    turned = jnp.concatenate([turned, turned], 1)
+    items = []
+    for source in range(cols_y):
+        for block in range(blocks):
+            flipped = held_ref[source, block].T
+            items.append(
+                jnp.concatenate(
+                    [flipped[j * channels : (j + 1) * channels] for j in range(groups)], 1
+                )
+            )
+    high, low = halves(jnp.concatenate(items, 1))
+    points = matmul(turned, jnp.concatenate([high, low], 0))
+    for source in range(cols_y):
+        for block in range(blocks):
+            tile = codes_ref[source, blocks + block, mine_y]
+            item = source * blocks + block
+
+            @pl.when(tile >= 0)
+            def _():
+                before[tile] += points[:, item * NZ : (item + 1) * NZ]
+
+    for piece in range(pieces):
+        value = back_ref[piece].reshape(cols_y * 2 * CX * CY, width)
+        value = jnp.concatenate([value] * (LANES // width), 1)
         for shift in range(groups):
-            rolled[lane_tile, shift] = (
-                pltpu.roll(part, shift * channels, 1) if shift else part
-            )
+            rolled[piece, shift] = pltpu.roll(value, shift * channels, 1) if shift else value
     spans = 2 * cols_y
     lane = lax.broadcasted_iota(jnp.int32, (spans, LANES), 1) // channels
-    bias = b_point_ref[...]
+    root = math.sqrt(2.0 / math.pi)
+    moves = []
     for chunk in range(CX * CY // groups):
         rows = []
-        for q in range(own_q):
+        for q in range(pieces * each):
             found = jnp.zeros((spans, LANES), f32)
             for j in range(groups):
                 piece = rolled[
-                    q // groups,
-                    (j - q) % groups,
+                    q // each,
+                    (j - q % each) % groups,
                     pl.ds(chunk * groups + j, spans, stride=CX * CY),
                     :,
                 ]
                 found = jnp.where(lane == j, piece, found)
             rows.append(found)
-        table = jnp.concatenate(rows, 0)
-        high, low = halves(table)
         spectral = lax.dot_general(
-            jnp.concatenate([high, low, high], 0),
+            split_rows(jnp.concatenate(rows, 0)),
             inverse_ref[...],
             (((0,), (0,)), ((), ())),
             preferred_element_type=f32,
         )
         for j in range(groups):
-            before[chunk * groups + j] = spectral[j * channels : (j + 1) * channels] + bias
-    turned = w_point_ref[...].astype(f32).T.astype(bf16)
-    turned = jnp.concatenate([turned, turned], 1)
-    for source in range(cols_y):
-        for block in range(blocks):
-            tile = codes_ref[source, blocks + block, mine_y]
-
-            @pl.when(tile >= 0)
-            def _():
-                flipped = held_ref[source, block].T
-                item = jnp.concatenate(
-                    [flipped[j * channels : (j + 1) * channels] for j in range(groups)], 1
-                )
-                high, low = halves(item)
-                before[tile] += matmul(turned, jnp.concatenate([high, low], 0))
-
-    root = math.sqrt(2.0 / math.pi)
-    for tile in range(CX * CY):
-        x = before[tile]
-        half = 0.5 * x
-        bent = jnp.tanh(x * (root + (0.044715 * root) * (x * x)))
-        out_ref[tile // CY, tile % CY] = half + half * bent
+            tile = chunk * groups + j
+            x = spectral[j * channels : (j + 1) * channels] + (before[tile] + bias)
+            half = 0.5 * x
+            bent = jnp.tanh(x * (root + (0.044715 * root) * (x * x)))
+            done[tile // CY, tile % CY] = half + half * bent
+        at = (chunk * groups // CY, pl.ds(chunk * groups % CY, groups))
+        move = pltpu.make_async_copy(done.at[at], out_ref.at[at], out_sem.at[chunk])
+        move.start()
+        moves.append(move)
+    for move in moves:
+        move.wait()
 
 
 def decoder(codes, held, back, inverse, w_point, b_point):
     smem = pl.BlockSpec(memory_space=pltpu.SMEM)
     vmem = pl.BlockSpec(memory_space=pltpu.VMEM)
     channels = w_point.shape[0]
-    lane_tiles = max(1, back.shape[2] // LANES)
-    rows = back.shape[0] * back.shape[1]
+    rows = back.shape[1] * back.shape[2]
+    shape = (CX, CY, channels, NZ)
     return pl.pallas_call(
         decoder_kernel,
-        out_shape=jax.ShapeDtypeStruct((CX, CY, channels, NZ), f32),
+        out_shape=jax.ShapeDtypeStruct(shape, f32),
         in_specs=[smem] + [vmem] * 5,
-        out_specs=vmem,
+        out_specs=pl.BlockSpec(memory_space=pl.ANY),
         scratch_shapes=[
-            pltpu.VMEM((lane_tiles, LANES // channels, rows, LANES), f32),
+            pltpu.VMEM((back.shape[0], LANES // channels, rows, LANES), f32),
             pltpu.VMEM((CX * CY, channels, NZ), f32),
+            pltpu.VMEM(shape, f32),
+            pltpu.SemaphoreType.DMA((CX * CY * channels // LANES,)),
         ],
         name="decoder",
-    )(codes, held, back, inverse, w_point, b_point[:, None])
+    )(codes, held, back, inverse, w_point, b_point[None])
 
 
 def local(

time: 54.7 us -> 48.7 us (0.89)
  Pallas kernels: 52.6 us -> 48.5 us
  local copies, waits for them, and re-layouts: 1.34 us -> 0 us
    pallas_call x1, Pallas kernels: 48.1 us -> 45.1 us  [encoder(): pl.pallas_call(encoder_kernel, out_shape=(jax.ShapeDtypeStruct((cols_y, 8...]
    broadcast_in_dim x1 -> x0, local copies, waits for them, and re-layouts: 1.34 us -> none  [decoder(): b_point[:, None]]
    pallas_call x1, Pallas kernels: 4.53 us -> 3.4 us  [decoder(): pl.pallas_call(decoder_kernel, out_shape=jax.ShapeDtypeStruct(shape, f32)...]
where the time goes in v2:
time: 48.7 us; the launch traced here: 48.5 us
  Pallas kernels  48.5 us (100%)
    pallas_call x1, Pallas kernels, encoder(): pl.pallas_call(encoder_kernel, out_shape=(jax.ShapeDtypeStruct((cols_y, 8...  45.1 us
    pallas_call x1, Pallas kernels, decoder(): pl.pallas_call(decoder_kernel, out_shape=jax.ShapeDtypeStruct(shape, f32)...  3.4 us

profile of v2, /device:TPU:0, one launch (start us, length us, event | category | flops | bytes accessed | tf_op | source)
XLA Modules:
  0.0 48.5 jit_solution(3950408045546731734)
XLA Ops:
  0.0 45.1 %encoder.1 = (s32[4,8,128]{2,1,0:T(8,128)}, f32[4,2,32,128]{3,2,1,0:T(8,128)}, f32[2,4,64,128]{3,2,1,0:T(8,128)}) custom-call(s32[2,4]{1,0:T(2,128)} %owner_ref.1, s32[2,4]{1,0:T(2,128)} %local_ref.1, s32[2]{0:T(128)} %live_ref.1, bf16[32,256]{1,0:T(8,128)(2,1)} %features_ref.1, bf16[3,256]{1,0:T(4,128)(2,1)} %offsets_ref.1, s32[1,256]{1,0:T(1,128)} %bitcast.5, ...), custom_call_target="tpu_custom_call" | custom-call | tf_op jit(solution)/shard_map/encoder/pallas_call | solution.py:531
  45.1 3.4 %decoder.1 = f32[4,8,32,128]{3,2,1,0:T(8,128)} custom-call(s32[4,8,128]{2,1,0:T(8,128)} %get-tuple-element.8.codes_ref, f32[4,2,32,128]{3,2,1,0:T(8,128)} %get-tuple-element.9.held_ref, f32[2,4,64,128]{3,2,1,0:T(8,128)} %get-tuple-element.10.back_ref, bf16[192,128]{1,0:T(8,128)(2,1)} %constant.11.clone.inverse_ref, bf16[32,32]{1,0:T(8,128)(2,1)} %w_point_ref.1, ...), custom_call_target="tpu_custom_call" | custom-call | tf_op jit(solution)/shard_map/decoder/pallas_call | solution.py:679

commit v3 on v2

--- a/solution.py
+++ b/solution.py
@@ -16,7 +16,7 @@
 LANES = 128
 
 GROUP = 4
-UNROLL = 8
+UNROLL = 16
 
 LINEAR = 2.0 * math.sqrt(2.0 / math.pi)
 CUBIC = 4.0 * 0.044715 * LINEAR
@@ -79,6 +79,12 @@
     return split_table(z_table), split_table(backward), split_table(lift), inverse
 
 
+def parts_of(blocks, listed):
+    whole = [(block, 0, listed) for block in range(blocks - 1)]
+    half = listed // 2
+    return whole + [(blocks - 1, 0, half), (blocks - 1, half, listed - half)]
+
+
 def encoder_kernel(
     owner_ref,
     local_ref,
@@ -92,13 +98,15 @@
     b_second_ref,
     w_third_ref,
     z_table_ref,
-    backward_ref,
-    lift_ref,
+    backward_hbm,
+    lift_hbm,
     modes_ref,
     codes_ref,
     held_ref,
     back_ref,
     weights,
+    backward_ref,
+    lift_ref,
     cell_sin,
     cell_cos,
     point_sin,
@@ -108,6 +116,7 @@
     feats,
     second,
     sums,
+    dense,
     code_sent,
     code_got,
     sent_a,
@@ -135,8 +144,13 @@
     two = 2 * hid
     quarter = PB // GROUP
     size_x, size_y = CX * cols_x, CY * cols_y
-    load = pltpu.make_async_copy(modes_ref, weights, load_sem)
-    load.start()
+    loads = []
+    for index, (source, target) in enumerate(
+        ((modes_ref, weights), (backward_hbm, backward_ref), (lift_hbm, lift_ref))
+    ):
+        load = pltpu.make_async_copy(source, target, load_sem.at[index])
+        load.start()
+        loads.append(load)
 
     def everyone(body):
         if count <= 32:
@@ -196,11 +210,14 @@
     base_sin, base_cos = jnp.sin(base), jnp.cos(base)
     code_lane = lax.broadcasted_iota(jnp.int32, (1, LANES), 1)
     code_rows = []
-    for block in range(blocks):
+    parts = parts_of(blocks, listed)
+    for block, begin, some in parts:
         row = jnp.zeros((1, LANES), jnp.int32)
-        for slot in range(listed):
-            code = owner_ref[block, slot] * (CX * CY) + local_ref[block, slot]
-            row = jnp.where(code_lane % listed == slot, code, row)
+        for slot in range(some):
+            code = (
+                owner_ref[block, begin + slot] * (CX * CY) + local_ref[block, begin + slot]
+            )
+            row = jnp.where(code_lane % some == slot, code, row)
         code_rows.append(row)
     for block in range(blocks):
         row = jnp.full((1, LANES), -1, jnp.int32)
@@ -208,15 +225,32 @@
             alive = jnp.where(slot < live_ref[block], local_ref[block, slot], -1)
             row = jnp.where(code_lane == owner_ref[block, slot], alive, row)
         code_rows.append(row)
-    code_rows.append(jnp.zeros((8 - 2 * blocks, LANES), jnp.int32))
+    code_rows.append(jnp.zeros((8 - len(code_rows), LANES), jnp.int32))
     code_sent[...] = jnp.concatenate(code_rows, 0)
 
     lane = lax.broadcasted_iota(jnp.int32, (quarter, two), 1)
 
-    def pairs(block):
+    def points(block):
         here = slice(block * PB, (block + 1) * PB)
-        for slot in range(listed):
-            item = block * listed + slot
+        spots = places[:, here].T
+        for half in range(GROUP // 2):
+            low = slice(2 * half * quarter, (2 * half + 1) * quarter)
+            up = slice((2 * half + 1) * quarter, (2 * half + 2) * quarter)
+            cols = slice(half * two, (half + 1) * two)
+            side = 0.0
+            for axis in range(3):
+                spot = jnp.where(lane < hid, spots[low, axis : axis + 1], spots[up, axis : axis + 1])
+                side = side + double_first[axis : axis + 1] * spot
+            point_cos[:, cols] = jnp.cos(side)
+            point_sin[:, cols] = jnp.sin(side)
+        turned = features[:, here].T
+        feats[...] = jnp.concatenate(
+            [turned[j * quarter : (j + 1) * quarter] for j in range(GROUP)], 1
+        )
+
+    def pairs(block, begin, some):
+        for slot in range(some):
+            item = block * listed + begin + slot
             b_sin, b_cos = base_sin[item : item + 1], base_cos[item : item + 1]
             near_sin = sin_fine * b_cos + cos_fine * b_sin
             near_cos = cos_fine * b_cos - sin_fine * b_sin
@@ -225,23 +259,6 @@
                 far_cos, far_sin = cosine[step : step + 1], sine[step : step + 1]
                 cell_sin[rows, :] = far_cos * near_sin + far_sin * near_cos
                 cell_cos[rows, :] = far_cos * near_cos - far_sin * near_sin
-        spots = places[:, here].T
-        side = (
-            double_first[0:1] * spots[:, 0:1]
-            + double_first[1:2] * spots[:, 1:2]
-            + double_first[2:3] * spots[:, 2:3]
-        )
-        side_cos, side_sin = jnp.cos(side), jnp.sin(side)
-        for half in range(GROUP // 2):
-            low = slice(2 * half * quarter, (2 * half + 1) * quarter)
-            up = slice((2 * half + 1) * quarter, (2 * half + 2) * quarter)
-            cols = slice(half * two, (half + 1) * two)
-            point_cos[:, cols] = jnp.where(lane < hid, side_cos[low], side_cos[up])
-            point_sin[:, cols] = jnp.where(lane < hid, side_sin[low], side_sin[up])
-        turned = features[:, here].T
-        feats[...] = jnp.concatenate(
-            [turned[j * quarter : (j + 1) * quarter] for j in range(GROUP)], 1
-        )
         sums[...] = jnp.zeros_like(sums)
 
         @pl.loop(0, quarter // UNROLL)
@@ -256,7 +273,7 @@
                     spread_three[
                         rows, LANES + part * channels : LANES + (part + 1) * channels
                     ] = rest[:, cols]
-            for slot in range(listed):
+            for slot in range(some):
                 rows = slice(slot * NZ, (slot + 1) * NZ)
                 for inner in range(UNROLL):
                     group = step * UNROLL + inner
@@ -277,33 +294,33 @@
     lane_r = lax.broadcasted_iota(jnp.int32, (quarter, LANES), 1) // channels
     scale = 1.0 / math.sqrt(PB)
 
-    def parcels(block):
+    def parcels(part):
+        block, begin, some = parts[part]
         flat = jnp.zeros((NZ, LANES), f32)
-        dense = []
-        for slot in range(listed):
+        for slot in range(some):
             rows = slice(slot * NZ, (slot + 1) * NZ)
             total = sums[rows, 0:LANES] + sums[rows, LANES:]
             total = total + pltpu.roll(total, 2 * channels, 1)
             total = total + pltpu.roll(total, channels, 1)
-            total = jnp.where(slot < live_ref[block], total * scale, 0.0)
+            total = jnp.where(begin + slot < live_ref[block], total * scale, 0.0)
             flat = jnp.where(lane_z == slot, total, flat)
             tight = total[0:quarter]
-            for part in range(1, GROUP):
-                tight = jnp.where(
-                    lane_r == part, total[part * quarter : (part + 1) * quarter], tight
-                )
-            dense.append(tight)
+            for at in range(1, GROUP):
+                tight = jnp.where(lane_r == at, total[at * quarter : (at + 1) * quarter], tight)
+            dense[begin + slot] = tight
         modes = matmul(z_table_ref[...], split_rows(flat))
         span = 2 * cols_y
-        for slot in range(listed):
+        for slot in range(some):
             lanes = slice(slot * channels, (slot + 1) * channels)
             joined = jnp.concatenate(
                 [modes[q * span : (q + 1) * span, lanes] for q in range(own_q)], 1
             )
-            for part in range(2):
-                sent_a[block, :, part * listed + slot, :] = joined[
-                    part * cols_y : (part + 1) * cols_y
+            for half in range(2):
+                sent_a[part, :, half * some + slot, :] = joined[
+                    half * cols_y : (half + 1) * cols_y
                 ]
+
+    def raws(block):
         for dest in range(cols_y):
             chosen = jnp.zeros((quarter, LANES), f32)
             for slot in range(listed):
@@ -322,13 +339,15 @@
     def keep(source, target, stage):
         pltpu.make_async_copy(source, target, recvs.at[stage]).start()
 
-    def spread(block):
+    def spread(part):
+        rows = pl.ds(0, 2 * parts[part][2])
+
         def go(step):
             x, y = place(step)
-            send(sent_a.at[block, y], got_a.at[block, me], block, x, y)
+            send(sent_a.at[part, y, rows], got_a.at[part, me, rows], part, x, y)
 
         everyone(go)
-        keep(sent_a.at[block, mine_y], got_a.at[block, me], block)
+        keep(sent_a.at[part, mine_y, rows], got_a.at[part, me, rows], part)
 
     def arrive(target, stage):
         pltpu.make_async_copy(target, target, recvs.at[stage]).wait()
@@ -336,24 +355,27 @@
     def depart(part, stage):
         pltpu.make_async_copy(part, part, sends.at[stage]).wait()
 
-    stage_code, stage_raw, stage_d = blocks, blocks + 1, blocks + 2
+    stage_code = len(parts)
+    stage_raw, stage_d = stage_code + 1, stage_code + 2
     stage_e = stage_d + sent_d.shape[0]
 
-    pairs(0)
-    parcels(0)
-    pl.semaphore_wait(barrier, count - 1)
-
-    def tell(step):
-        x, y = place(step)
-        send(code_sent, code_got.at[me], stage_code, x, y)
-
-    everyone(tell)
-    keep(code_sent, code_got.at[me], stage_code)
-    spread(0)
-    for block in range(1, blocks):
-        pairs(block)
-        parcels(block)
-        spread(block)
+    for part, (block, begin, some) in enumerate(parts):
+        if begin == 0:
+            points(block)
+        pairs(block, begin, some)
+        parcels(part)
+        if part == 0:
+            pl.semaphore_wait(barrier, count - 1)
+
+            def tell(step):
+                x, y = place(step)
+                send(code_sent, code_got.at[me], stage_code, x, y)
+
+            everyone(tell)
+            keep(code_sent, code_got.at[me], stage_code)
+        spread(part)
+        if begin + some == listed:
+            raws(block)
 
     for step in range(1, cols_y):
         other = lax.rem(mine_y + step, cols_y)
@@ -363,53 +385,61 @@
     arrive(code_got, stage_code)
     own_p = sent_d.shape[2] // (2 * CX)
     modes = own_p * cols_x
-    each = 2 * listed
-    depth = count * each
-    column = lax.broadcasted_iota(jnp.int32, (1, depth), 1)
-    source = column // each
     slots = modes * 2
-    row = lax.broadcasted_iota(jnp.int32, (slots, depth), 0)
-    which = (row // 8) * 4 + row % 4
-    freq_x = jnp.where(which < modes // 2, which, size_x - modes + which)
-    part_out = (row // 4) % 2
-    part_in = (column // listed) % 2
-    quarters = (part_out - part_in).astype(f32) * 0.25
-    p_at = mine_x * own_p + lax.broadcasted_iota(jnp.int32, (own_p, depth), 0)
-    freq_y = jnp.where(p_at < modes // 2, p_at, size_y - modes + p_at)
-    owns = (
-        lax.broadcasted_iota(jnp.int32, (count, depth), 1) // each
-        == lax.broadcasted_iota(jnp.int32, (count, depth), 0)
-    )
+    lanes_w = got_a.shape[3]
 
     def waves(turns):
         angle = (turns - jnp.floor(turns)) * (2.0 * math.pi)
         return jnp.cos(angle), jnp.sin(angle)
 
-    for block in range(blocks):
-        codes = jnp.concatenate([code_got[:, block, :].astype(f32)] * (depth // LANES), 1)
+    starts = [0]
+    for part, (block, begin, some) in enumerate(parts):
+        each = 2 * some
+        depth = count * each
+        column = lax.broadcasted_iota(jnp.int32, (1, depth), 1)
+        source = column // each
+        row = lax.broadcasted_iota(jnp.int32, (slots, depth), 0)
+        which = (row // 8) * 4 + row % 4
+        freq_x = jnp.where(which < modes // 2, which, size_x - modes + which)
+        part_out = (row // 4) % 2
+        part_in = (column // some) % 2
+        quarters = (part_out - part_in).astype(f32) * 0.25
+        p_at = mine_x * own_p + lax.broadcasted_iota(jnp.int32, (own_p, depth), 0)
+        freq_y = jnp.where(p_at < modes // 2, p_at, size_y - modes + p_at)
+        owns = (
+            lax.broadcasted_iota(jnp.int32, (count, depth), 1) // each
+            == lax.broadcasted_iota(jnp.int32, (count, depth), 0)
+        )
+        codes = jnp.concatenate([code_got[:, part, :].astype(f32)] * (depth // LANES), 1)
         code = jnp.sum(jnp.where(owns, codes, 0.0), axis=0, keepdims=True).astype(jnp.int32)
         tile = code % (CX * CY)
         x_at = CX * (source // cols_y) + tile // CY
         y_at = CY * (code // (CX * CY)) + tile % CY
         x_cos, x_sin = waves((freq_x * x_at).astype(f32) * (1.0 / size_x) + quarters)
         y_cos, y_sin = waves((freq_y * y_at).astype(f32) * (1.0 / size_y))
+        start = starts[part]
         for p in range(own_p):
             value = x_cos * y_cos[p : p + 1] - x_sin * y_sin[p : p + 1]
             high, low = halves(value)
             rows = slice(p * slots, (p + 1) * slots)
-            start = block * 3 * depth
             phases[rows, start : start + depth] = high
             phases[rows, start + depth : start + 2 * depth] = high
             phases[rows, start + 2 * depth : start + 3 * depth] = low
-    lanes_w = got_a.shape[3]
-    for block in range(blocks):
-        arrive(got_a.at[block], block)
-        splits[block * 3 * depth : (block + 1) * 3 * depth, :] = split_rows(
-            got_a[block].reshape(depth, lanes_w)
+        starts.append(start + 3 * depth)
+    for part, (block, begin, some) in enumerate(parts):
+        rows = pl.ds(0, 2 * some)
+        arrive(got_a.at[part, :, rows], part)
+        splits[starts[part] : starts[part + 1], :] = split_rows(
+            got_a[part, :, 0 : 2 * some].reshape(count * 2 * some, lanes_w)
         )
-    spectra[...] = matmul(phases[...], splits[...])
-
-    load.wait()
+        if part == len(parts) - 2:
+            seen = slice(0, starts[part + 1])
+            spectra[...] = matmul(phases[:, seen], splits[seen, :])
+    seen = slice(starts[-2], starts[-1])
+    spectra[...] += matmul(phases[:, seen], splits[seen, :])
+
+    for load in loads:
+        load.wait()
     pieces, width = sent_d.shape[0], sent_d.shape[3]
     quad = 8 * channels
     bands = LANES // channels
@@ -481,8 +511,8 @@
             )
         keep(sent_e.at[piece, mine_y], back_ref.at[piece, mine_y], stage_e + piece)
     codes_ref[...] = code_got[pl.ds(mine_x * cols_y, cols_y)]
-    for block in range(blocks):
-        depart(got_a.at[block, pl.ds(0, count - 1)], block)
+    for part, (block, begin, some) in enumerate(parts):
+        depart(got_a.at[part, pl.ds(0, count - 1), pl.ds(0, 2 * some)], part)
     depart(code_got.at[pl.ds(0, count - 1)], stage_code)
     depart(raw_sent.at[pl.ds(0, cols_y - 1)], stage_raw)
     for piece in range(pieces):
@@ -525,9 +555,11 @@
     vmem = pl.BlockSpec(memory_space=pltpu.VMEM)
     pieces = max(1, lanes // LANES)
     width = lanes // pieces
+    anywhere = pl.BlockSpec(memory_space=pl.ANY)
     last = (pieces, cols_y, 2 * CX * CY, width)
     parcel = (pieces, cols_x, 2 * own_p * CX, width)
-    stages = blocks + 2 + 2 * pieces
+    number = len(parts_of(blocks, listed))
+    stages = number + 2 + 2 * pieces
     return pl.pallas_call(
         encoder_kernel,
         out_shape=(
@@ -535,10 +567,12 @@
             jax.ShapeDtypeStruct((cols_y, blocks, quarter, LANES), f32),
             jax.ShapeDtypeStruct(last, f32),
         ),
-        in_specs=[smem] * 3 + [vmem] * 11 + [pl.BlockSpec(memory_space=pl.ANY)],
-        out_specs=(vmem, vmem, vmem),
+        in_specs=[smem] * 3 + [vmem] * 9 + [anywhere] * 3,
+        out_specs=(vmem, anywhere, anywhere),
         scratch_shapes=[
             pltpu.VMEM(w_modes.shape, w_modes.dtype),
+            pltpu.VMEM(backward.shape, backward.dtype),
+            pltpu.VMEM(lift.shape, lift.dtype),
             pltpu.VMEM((listed * NZ, 2 * hid), f32),
             pltpu.VMEM((listed * NZ, 2 * hid), f32),
             pltpu.VMEM((quarter, wide), f32),
@@ -548,10 +582,11 @@
             pltpu.VMEM((quarter, GROUP * channels), f32),
             pltpu.VMEM((listed * NZ, UNROLL * wide), bf16),
             pltpu.VMEM((listed * NZ, 2 * GROUP * channels), f32),
+            pltpu.VMEM((listed, quarter, LANES), f32),
             pltpu.VMEM((8, LANES), jnp.int32),
             pltpu.VMEM((count, 8, LANES), jnp.int32),
-            pltpu.VMEM((blocks, cols_y, 2 * listed, lanes), f32),
-            pltpu.VMEM((blocks, count, 2 * listed, lanes), f32),
+            pltpu.VMEM((number, cols_y, 2 * listed, lanes), f32),
+            pltpu.VMEM((number, count, 2 * listed, lanes), f32),
             pltpu.VMEM((cols_y, blocks, quarter, LANES), f32),
             pltpu.VMEM((slots, blocks * 3 * depth), bf16),
             pltpu.VMEM((blocks * 3 * depth, lanes), bf16),
@@ -560,7 +595,7 @@
             pltpu.VMEM(parcel, f32),
             pltpu.VMEM(parcel, f32),
             pltpu.VMEM(last, f32),
-            pltpu.SemaphoreType.DMA,
+            pltpu.SemaphoreType.DMA((3,)),
             pltpu.SemaphoreType.DMA((stages,)),
             pltpu.SemaphoreType.DMA((stages,)),
         ],
@@ -601,6 +636,7 @@
     cols_y, blocks, quarter = held_ref.shape[:3]
     channels = w_point_ref.shape[0]
     mine_y = lax.axis_index("gy")
+    codes_at = len(parts_of(blocks, GROUP))
     groups = LANES // channels
     pieces, width = back_ref.shape[0], back_ref.shape[3]
     each = width // channels
@@ -621,7 +657,7 @@
     points = matmul(turned, jnp.concatenate([high, low], 0))
     for source in range(cols_y):
         for block in range(blocks):
-            tile = codes_ref[source, blocks + block, mine_y]
+            tile = codes_ref[source, codes_at + block, mine_y]
             item = source * blocks + block
 
             @pl.when(tile >= 0)

time: 48.7 us -> 47.4 us (0.973)
  Pallas kernels: 48.5 us -> 47.2 us
    pallas_call x1, Pallas kernels: 45.1 us -> 43.8 us  [encoder(): pl.pallas_call(encoder_kernel, out_shape=(jax.ShapeDtypeStruct((cols_y, 8...]
where the time goes in v3:
time: 47.4 us; the launch traced here: 47.2 us
  Pallas kernels  47.2 us (100%)
    pallas_call x1, Pallas kernels, encoder(): pl.pallas_call(encoder_kernel, out_shape=(jax.ShapeDtypeStruct((cols_y, 8...  43.8 us
    pallas_call x1, Pallas kernels, decoder(): pl.pallas_call(decoder_kernel, out_shape=jax.ShapeDtypeStruct(shape, f32)...  3.4 us

profile of v3, /device:TPU:0, one launch (start us, length us, event | category | flops | bytes accessed | tf_op | source)
XLA Modules:
  0.0 47.2 jit_solution(4847098412772807914)
XLA Ops:
  0.0 43.8 %encoder.1 = (s32[4,8,128]{2,1,0:T(8,128)}, f32[4,2,32,128]{3,2,1,0:T(8,128)}, f32[2,4,64,128]{3,2,1,0:T(8,128)}) custom-call(s32[2,4]{1,0:T(2,128)} %owner_ref.1, s32[2,4]{1,0:T(2,128)} %local_ref.1, s32[2]{0:T(128)} %live_ref.1, bf16[32,256]{1,0:T(8,128)(2,1)} %features_ref.1, bf16[3,256]{1,0:T(4,128)(2,1)} %offsets_ref.1, s32[1,256]{1,0:T(1,128)} %bitcast.5, ...), custom_call_target="tpu_custom_call" | custom-call | tf_op jit(solution)/shard_map/encoder/pallas_call | solution.py:563
  43.8 3.4 %decoder.1 = f32[4,8,32,128]{3,2,1,0:T(8,128)} custom-call(s32[4,8,128]{2,1,0:T(8,128)} %get-tuple-element.8.codes_ref, f32[4,2,32,128]{3,2,1,0:T(8,128)} %get-tuple-element.9.held_ref, f32[2,4,64,128]{3,2,1,0:T(8,128)} %get-tuple-element.10.back_ref, bf16[192,128]{1,0:T(8,128)(2,1)} %constant.11.clone.inverse_ref, bf16[32,32]{1,0:T(8,128)(2,1)} %w_point_ref.1, ...), custom_call_target="tpu_custom_call" | custom-call | tf_op jit(solution)/shard_map/decoder/pallas_call | solution.py:715

commit v4 on v3

--- a/solution.py
+++ b/solution.py
@@ -70,13 +70,13 @@
     inverse = np.concatenate([high, high, low], 0)
     x_turns = 2 * np.pi * (np.outer(frequencies(size_x), np.arange(size_x)) % size_x) / size_x
     backward = turn(x_turns).reshape(2, 2, modes // 4, 4, cols_x, CX)
-    backward = np.einsum("srgkdx,pP->dsPxpgrk", backward, np.eye(own_p))
-    backward = backward.reshape(-1, modes * 2 * own_p)
+    backward = np.einsum("srgkdx->dsxgrk", backward).reshape(-1, modes * 2)
     y_turns = 2 * np.pi * (np.outer(frequencies(size_y), np.arange(size_y)) % size_y) / size_y
     lift = turn(y_turns).reshape(2, 2, cols_x, own_p, cols_y, CY)
-    lift = np.einsum("srepdy,xX->dsxyerpX", lift, np.eye(CX))
-    lift = lift.reshape(2 * CX * size_y, -1)
-    return split_table(z_table), split_table(backward), split_table(lift), inverse
+    lift = np.einsum("srepdy,xX->pdsxyerX", lift, np.eye(CX))
+    lift = lift.reshape(own_p, 2 * CX * size_y, -1)
+    lift = np.stack([split_table(each) for each in lift], 0)
+    return split_table(z_table), split_table(backward), lift, inverse
 
 
 def parts_of(blocks, listed):
@@ -126,6 +126,7 @@
     splits,
     spectra,
     mixed,
+    lifted,
     sent_d,
     got_d,
     sent_e,
@@ -152,21 +153,30 @@
         load.start()
         loads.append(load)
 
+    def around(mine, step, size):
+        other = mine + step
+        return jnp.where(other >= size, other - size, other)
+
+    near_x = [around(mine_x, step, cols_x) for step in range(cols_x)]
+    near_y = [around(mine_y, step, cols_y) for step in range(cols_y)]
+
     def everyone(body):
         if count <= 32:
-            for step in range(1, count):
-                body(step)
+            for x in near_x:
+                for y in near_y:
+                    if x is not near_x[0] or y is not near_y[0]:
+                        body(x, y)
         else:
-            pl.loop(1, count)(body)
-
-    def place(step):
-        other = lax.rem(me + step, count)
-        return other // cols_y, lax.rem(other, cols_y)
+
+            @pl.loop(1, count)
+            def _(step):
+                other = lax.rem(me + step, count)
+                x = lax.div(other, cols_y)
+                body(x, other - x * cols_y)
 
     barrier = pltpu.get_barrier_semaphore()
 
-    def greet(step):
-        x, y = place(step)
+    def greet(x, y):
         pl.semaphore_signal(barrier, inc=1, device_id={"gx": x, "gy": y})
 
     everyone(greet)
@@ -342,8 +352,7 @@
     def spread(part):
         rows = pl.ds(0, 2 * parts[part][2])
 
-        def go(step):
-            x, y = place(step)
+        def go(x, y):
             send(sent_a.at[part, y, rows], got_a.at[part, me, rows], part, x, y)
 
         everyone(go)
@@ -367,8 +376,7 @@
         if part == 0:
             pl.semaphore_wait(barrier, count - 1)
 
-            def tell(step):
-                x, y = place(step)
+            def tell(x, y):
                 send(code_sent, code_got.at[me], stage_code, x, y)
 
             everyone(tell)
@@ -377,13 +385,8 @@
         if begin + some == listed:
             raws(block)
 
-    for step in range(1, cols_y):
-        other = lax.rem(mine_y + step, cols_y)
-        send(raw_sent.at[other], held_ref.at[mine_y], stage_raw, mine_x, other)
-    keep(raw_sent.at[mine_y], held_ref.at[mine_y], stage_raw)
-
     arrive(code_got, stage_code)
-    own_p = sent_d.shape[2] // (2 * CX)
+    own_p = sent_d.shape[0]
     modes = own_p * cols_x
     slots = modes * 2
     lanes_w = got_a.shape[3]
@@ -438,9 +441,13 @@
     seen = slice(starts[-2], starts[-1])
     spectra[...] += matmul(phases[:, seen], splits[seen, :])
 
+    for step in range(1, cols_y):
+        other = near_y[step]
+        send(raw_sent.at[other], held_ref.at[mine_y], stage_raw, mine_x, other)
+    keep(raw_sent.at[mine_y], held_ref.at[mine_y], stage_raw)
+
     for load in loads:
         load.wait()
-    pieces, width = sent_d.shape[0], sent_d.shape[3]
     quad = 8 * channels
     bands = LANES // channels
     row_of = lax.broadcasted_iota(jnp.int32, (8, LANES), 0)
@@ -449,59 +456,51 @@
     own_four = [row_of % 4 == 2 * side + lane_of // (2 * channels) for side in range(2)]
     negate = row_of < 4
     fours = modes // 4
-    ahead = 8
-
-    for piece in range(pieces):
-        first_q = piece * (width // channels)
-
-        @pl.loop(0, own_p * fours // ahead)
-        def _(outer):
-            for inner in range(ahead):
-                group = outer * ahead + inner
-                p = group // fours
-                low = (group % fours) * 4
-                start = pl.multiple_of(group * 8, 8)
-                plain = spectra[pl.ds(start, 8), piece * width : (piece + 1) * width]
-                plain = jnp.concatenate([plain] * (LANES // width), 1)
+    tiles = max(1, lanes_w // LANES)
+    width = lanes_w // tiles
+    each = width // channels
+    for p in range(own_p):
+        for group in range(fours):
+            rows = slice((p * fours + group) * 8, (p * fours + group) * 8 + 8)
+            for at_tile in range(tiles):
+                cols = slice(at_tile * width, (at_tile + 1) * width)
+                plain = jnp.concatenate([spectra[rows, cols]] * (LANES // width), 1)
                 turned = pltpu.roll(plain, 4, 0)
                 turned = jnp.where(negate, -turned, turned)
                 plains = [plain] + [pltpu.roll(plain, r * channels, 1) for r in range(1, bands)]
                 turns = [turned] + [pltpu.roll(turned, r * channels, 1) for r in range(1, bands)]
                 outs = []
-                for q in range(width // channels):
+                for q in range(each):
                     both = plains[-q % bands]
                     for at in range(1, bands):
                         kind = turns if at % 2 else plains
                         both = jnp.where(band == at, kind[(at - q) % bands], both)
                     both = jnp.concatenate([jnp.where(own, both, 0.0) for own in own_four], 1)
                     high, rest = halves(both)
-                    tile = weights[pl.ds(low, 4), p, first_q + q].reshape(quad, channels)
-                    out = matmul(jnp.concatenate([high, rest], 0), tile)
+                    tile = weights[group * 4 : group * 4 + 4, p, at_tile * each + q]
+                    out = matmul(jnp.concatenate([high, rest], 0), tile.reshape(quad, channels))
                     outs.append(out[:8] + out[8:])
-                mixed[pl.ds(start, 8), piece * width : (piece + 1) * width] = jnp.concatenate(
-                    outs, 1
-                )
-
-        along_x = matmul(
-            backward_ref[...], split_rows(mixed[:, piece * width : (piece + 1) * width])
-        )
-        sent_d[piece] = along_x.reshape(sent_d.shape[1:])
+                mixed[group * 8 : group * 8 + 8, cols] = jnp.concatenate(outs, 1)
+        along_x = matmul(backward_ref[...], split_rows(mixed[...]))
+        sent_d[p] = along_x.reshape(sent_d.shape[1:])
         for step in range(1, cols_x):
-            other = lax.rem(mine_x + step, cols_x)
-            send(
-                sent_d.at[piece, other],
-                got_d.at[piece, mine_x],
-                stage_d + piece,
-                other,
-                mine_y,
-            )
-        keep(sent_d.at[piece, mine_x], got_d.at[piece, mine_x], stage_d + piece)
-    for piece in range(pieces):
-        arrive(got_d.at[piece], stage_d + piece)
-        along_y = matmul(lift_ref[...], split_rows(got_d[piece].reshape(-1, width)))
+            other = near_x[step]
+            send(sent_d.at[p, other], got_d.at[p, mine_x], stage_d + p, other, mine_y)
+        keep(sent_d.at[p, mine_x], got_d.at[p, mine_x], stage_d + p)
+    for p in range(own_p - 1):
+        arrive(got_d.at[p], stage_d + p)
+        part = matmul(lift_ref[p], split_rows(got_d[p].reshape(-1, lanes_w)))
+        lifted[...] = part if p == 0 else lifted[...] + part
+    p = own_p - 1
+    arrive(got_d.at[p], stage_d + p)
+    for piece in range(tiles):
+        cols = slice(piece * width, (piece + 1) * width)
+        along_y = matmul(lift_ref[p], split_rows(got_d[p, :, :, cols].reshape(-1, width)))
+        if p:
+            along_y = lifted[:, cols] + along_y
         sent_e[piece] = along_y.reshape(sent_e.shape[1:])
         for step in range(1, cols_y):
-            other = lax.rem(mine_y + step, cols_y)
+            other = near_y[step]
             send(
                 sent_e.at[piece, other],
                 back_ref.at[piece, mine_y],
@@ -515,10 +514,10 @@
         depart(got_a.at[part, pl.ds(0, count - 1), pl.ds(0, 2 * some)], part)
     depart(code_got.at[pl.ds(0, count - 1)], stage_code)
     depart(raw_sent.at[pl.ds(0, cols_y - 1)], stage_raw)
-    for piece in range(pieces):
-        depart(sent_d.at[piece, pl.ds(0, cols_x - 1)], stage_d + piece)
+    for p in range(own_p):
+        depart(sent_d.at[p, pl.ds(0, cols_x - 1)], stage_d + p)
     arrive(held_ref, stage_raw)
-    for piece in range(pieces):
+    for piece in range(tiles):
         arrive(back_ref.at[piece], stage_e + piece)
         depart(sent_e.at[piece, pl.ds(0, cols_y - 1)], stage_e + piece)
 
@@ -557,9 +556,9 @@
     width = lanes // pieces
     anywhere = pl.BlockSpec(memory_space=pl.ANY)
     last = (pieces, cols_y, 2 * CX * CY, width)
-    parcel = (pieces, cols_x, 2 * own_p * CX, width)
+    parcel = (own_p, cols_x, 2 * CX, lanes)
     number = len(parts_of(blocks, listed))
-    stages = number + 2 + 2 * pieces
+    stages = number + 2 + own_p + pieces
     return pl.pallas_call(
         encoder_kernel,
         out_shape=(
@@ -591,7 +590,8 @@
             pltpu.VMEM((slots, blocks * 3 * depth), bf16),
             pltpu.VMEM((blocks * 3 * depth, lanes), bf16),
             pltpu.VMEM((slots, lanes), f32),
-            pltpu.VMEM((slots, lanes), f32),
+            pltpu.VMEM((modes * 2, lanes), f32),
+            pltpu.VMEM((lift.shape[1], lanes), f32),
             pltpu.VMEM(parcel, f32),
             pltpu.VMEM(parcel, f32),
             pltpu.VMEM(last, f32),

time: 47.4 us -> 47.6 us (level)
  no operation moved by 1% of the time
where the time goes in v4:
time: 47.6 us; the launch traced here: 47.4 us
  Pallas kernels  47.2 us (99%)
    pallas_call x1, Pallas kernels, encoder(): pl.pallas_call(encoder_kernel, out_shape=(jax.ShapeDtypeStruct((cols_y, 8...  43.8 us
    pallas_call x1, Pallas kernels, decoder(): pl.pallas_call(decoder_kernel, out_shape=jax.ShapeDtypeStruct(shape, f32)...  3.37 us

profile of v4, /device:TPU:0, one launch (start us, length us, event | category | flops | bytes accessed | tf_op | source)
XLA Modules:
  0.0 47.4 jit_solution(11606984753467816600)
XLA Ops:
  0.0 43.8 %encoder.1 = (s32[4,8,128]{2,1,0:T(8,128)}, f32[4,2,32,128]{3,2,1,0:T(8,128)}, f32[2,4,64,128]{3,2,1,0:T(8,128)}) custom-call(s32[2,4]{1,0:T(2,128)} %owner_ref.1, s32[2,4]{1,0:T(2,128)} %local_ref.1, s32[2]{0:T(128)} %live_ref.1, bf16[32,256]{1,0:T(8,128)(2,1)} %features_ref.1, bf16[3,256]{1,0:T(4,128)(2,1)} %offsets_ref.1, s32[1,256]{1,0:T(1,128)} %bitcast.5, ...), custom_call_target="tpu_custom_call" | custom-call | tf_op jit(solution)/shard_map/encoder/pallas_call | solution.py:562
  43.8 3.4 %decoder.1 = f32[4,8,32,128]{3,2,1,0:T(8,128)} custom-call(s32[4,8,128]{2,1,0:T(8,128)} %get-tuple-element.8.codes_ref, f32[4,2,32,128]{3,2,1,0:T(8,128)} %get-tuple-element.9.held_ref, f32[2,4,64,128]{3,2,1,0:T(8,128)} %get-tuple-element.10.back_ref, bf16[192,128]{1,0:T(8,128)(2,1)} %constant.11.clone.inverse_ref, bf16[32,32]{1,0:T(8,128)(2,1)} %w_point_ref.1, ...), custom_call_target="tpu_custom_call" | custom-call | tf_op jit(solution)/shard_map/decoder/pallas_call | solution.py:715

commit v5 on v4

--- a/solution.py
+++ b/solution.py
@@ -121,6 +121,8 @@
     code_got,
     sent_a,
     got_a,
+    sent_b,
+    got_b,
     raw_sent,
     phases,
     splits,
@@ -350,6 +352,15 @@
         pltpu.make_async_copy(source, target, recvs.at[stage]).start()
 
     def spread(part):
+        if part == len(parts) - 1:
+            sent_b[...] = sent_a[part, :, 0 : sent_b.shape[1], :].astype(bf16)
+
+            def last(x, y):
+                send(sent_b.at[y], got_b.at[me], part, x, y)
+
+            everyone(last)
+            keep(sent_b.at[mine_y], got_b.at[me], part)
+            return
         rows = pl.ds(0, 2 * parts[part][2])
 
         def go(x, y):
@@ -425,19 +436,21 @@
             value = x_cos * y_cos[p : p + 1] - x_sin * y_sin[p : p + 1]
             high, low = halves(value)
             rows = slice(p * slots, (p + 1) * slots)
-            phases[rows, start : start + depth] = high
-            phases[rows, start + depth : start + 2 * depth] = high
-            phases[rows, start + 2 * depth : start + 3 * depth] = low
-        starts.append(start + 3 * depth)
-    for part, (block, begin, some) in enumerate(parts):
+            kinds = [high, low] if part == len(parts) - 1 else [high, high, low]
+            for index, kind in enumerate(kinds):
+                phases[rows, start + index * depth : start + (index + 1) * depth] = kind
+        starts.append(start + len(kinds) * depth)
+    for part, (block, begin, some) in enumerate(parts[:-1]):
         rows = pl.ds(0, 2 * some)
         arrive(got_a.at[part, :, rows], part)
         splits[starts[part] : starts[part + 1], :] = split_rows(
             got_a[part, :, 0 : 2 * some].reshape(count * 2 * some, lanes_w)
         )
-        if part == len(parts) - 2:
-            seen = slice(0, starts[part + 1])
-            spectra[...] = matmul(phases[:, seen], splits[seen, :])
+    seen = slice(0, starts[-2])
+    spectra[...] = matmul(phases[:, seen], splits[seen, :])
+    arrive(got_b, len(parts) - 1)
+    value = got_b[...].astype(f32).reshape(-1, lanes_w).astype(bf16)
+    splits[starts[-2] : starts[-1], :] = jnp.concatenate([value, value], 0)
     seen = slice(starts[-2], starts[-1])
     spectra[...] += matmul(phases[:, seen], splits[seen, :])
 
@@ -510,8 +523,9 @@
             )
         keep(sent_e.at[piece, mine_y], back_ref.at[piece, mine_y], stage_e + piece)
     codes_ref[...] = code_got[pl.ds(mine_x * cols_y, cols_y)]
-    for part, (block, begin, some) in enumerate(parts):
+    for part, (block, begin, some) in enumerate(parts[:-1]):
         depart(got_a.at[part, pl.ds(0, count - 1), pl.ds(0, 2 * some)], part)
+    depart(got_b.at[pl.ds(0, count - 1)], len(parts) - 1)
     depart(code_got.at[pl.ds(0, count - 1)], stage_code)
     depart(raw_sent.at[pl.ds(0, cols_y - 1)], stage_raw)
     for p in range(own_p):
@@ -586,6 +600,8 @@
             pltpu.VMEM((count, 8, LANES), jnp.int32),
             pltpu.VMEM((number, cols_y, 2 * listed, lanes), f32),
             pltpu.VMEM((number, count, 2 * listed, lanes), f32),
+            pltpu.VMEM((cols_y, 2 * (listed - listed // 2), lanes), bf16),
+            pltpu.VMEM((count, 2 * (listed - listed // 2), lanes), bf16),
             pltpu.VMEM((cols_y, blocks, quarter, LANES), f32),
             pltpu.VMEM((slots, blocks * 3 * depth), bf16),
             pltpu.VMEM((blocks * 3 * depth, lanes), bf16),
@@ -623,16 +639,20 @@
 def decoder_kernel(
     codes_ref,
     held_ref,
-    back_ref,
+    back_hbm,
     inverse_ref,
     w_point_ref,
     b_point_ref,
     out_ref,
+    back_ref,
     rolled,
     before,
     done,
     out_sem,
+    back_sem,
 ):
+    load = pltpu.make_async_copy(back_hbm, back_ref, back_sem)
+    load.start()
     cols_y, blocks, quarter = held_ref.shape[:3]
     channels = w_point_ref.shape[0]
     mine_y = lax.axis_index("gy")
@@ -664,6 +684,7 @@
             def _():
                 before[tile] += points[:, item * NZ : (item + 1) * NZ]
 
+    load.wait()
     for piece in range(pieces):
         value = back_ref[piece].reshape(cols_y * 2 * CX * CY, width)
         value = jnp.concatenate([value] * (LANES // width), 1)
@@ -715,13 +736,15 @@
     return pl.pallas_call(
         decoder_kernel,
         out_shape=jax.ShapeDtypeStruct(shape, f32),
-        in_specs=[smem] + [vmem] * 5,
+        in_specs=[smem, vmem, pl.BlockSpec(memory_space=pl.ANY)] + [vmem] * 3,
         out_specs=pl.BlockSpec(memory_space=pl.ANY),
         scratch_shapes=[
+            pltpu.VMEM(back.shape, f32),
             pltpu.VMEM((back.shape[0], LANES // channels, rows, LANES), f32),
             pltpu.VMEM((CX * CY, channels, NZ), f32),
             pltpu.VMEM(shape, f32),
             pltpu.SemaphoreType.DMA((CX * CY * channels // LANES,)),
+            pltpu.SemaphoreType.DMA,
         ],
         name="decoder",
     )(codes, held, back, inverse, w_point, b_point[None])

time: 47.6 us -> 46.9 us (0.985)
  Pallas kernels: 47.2 us -> 46.5 us
    pallas_call x1, Pallas kernels: 43.8 us -> 42.6 us  [encoder(): pl.pallas_call(encoder_kernel, out_shape=(jax.ShapeDtypeStruct((cols_y, 8...]
where the time goes in v5:
time: 46.9 us; the launch traced here: 46.6 us
  Pallas kernels  46.5 us (99%)
    pallas_call x1, Pallas kernels, encoder(): pl.pallas_call(encoder_kernel, out_shape=(jax.ShapeDtypeStruct((cols_y, 8...  42.6 us
    pallas_call x1, Pallas kernels, decoder(): pl.pallas_call(decoder_kernel, out_shape=jax.ShapeDtypeStruct(shape, f32)...  3.84 us

profile of v5, /device:TPU:0, one launch (start us, length us, event | category | flops | bytes accessed | tf_op | source)
XLA Modules:
  0.0 46.6 jit_solution(617723086210817907)
XLA Ops:
  0.0 42.6 %encoder.1 = (s32[4,8,128]{2,1,0:T(8,128)}, f32[4,2,32,128]{3,2,1,0:T(8,128)}, f32[2,4,64,128]{3,2,1,0:T(8,128)}) custom-call(s32[2,4]{1,0:T(2,128)} %owner_ref.1, s32[2,4]{1,0:T(2,128)} %local_ref.1, s32[2]{0:T(128)} %live_ref.1, bf16[32,256]{1,0:T(8,128)(2,1)} %features_ref.1, bf16[3,256]{1,0:T(4,128)(2,1)} %offsets_ref.1, s32[1,256]{1,0:T(1,128)} %bitcast.5, ...), custom_call_target="tpu_custom_call" | custom-call | tf_op jit(solution)/shard_map/encoder/pallas_call | solution.py:576
  42.6 3.8 %decoder.1 = f32[4,8,32,128]{3,2,1,0:T(8,128)} custom-call(s32[4,8,128]{2,1,0:T(8,128)} %get-tuple-element.8.codes_ref, f32[4,2,32,128]{3,2,1,0:T(8,128)} %get-tuple-element.9.held_ref, f32[2,4,64,128]{3,2,1,0:T(8,128)} %get-tuple-element.10.back_hbm, bf16[192,128]{1,0:T(8,128)(2,1)} %constant.11.clone.inverse_ref, bf16[32,32]{1,0:T(8,128)(2,1)} %w_point_ref.1, ...), custom_call_target="tpu_custom_call" | custom-call | tf_op jit(solution)/shard_map/decoder/pallas_call | solution.py:736

commit v6 on v5

--- a/solution.py
+++ b/solution.py
@@ -472,9 +472,10 @@
     tiles = max(1, lanes_w // LANES)
     width = lanes_w // tiles
     each = width // channels
-    for p in range(own_p):
+    @pl.loop(0, own_p)
+    def _(p):
         for group in range(fours):
-            rows = slice((p * fours + group) * 8, (p * fours + group) * 8 + 8)
+            rows = pl.ds(pl.multiple_of((p * fours + group) * 8, 8), 8)
             for at_tile in range(tiles):
                 cols = slice(at_tile * width, (at_tile + 1) * width)
                 plain = jnp.concatenate([spectra[rows, cols]] * (LANES // width), 1)
@@ -500,6 +501,7 @@
             other = near_x[step]
             send(sent_d.at[p, other], got_d.at[p, mine_x], stage_d + p, other, mine_y)
         keep(sent_d.at[p, mine_x], got_d.at[p, mine_x], stage_d + p)
+
     for p in range(own_p - 1):
         arrive(got_d.at[p], stage_d + p)
         part = matmul(lift_ref[p], split_rows(got_d[p].reshape(-1, lanes_w)))

time: 46.9 us -> 46.5 us (level)
  no operation moved by 1% of the time
where the time goes in v6:
time: 46.5 us; the launch traced here: 46.3 us
  Pallas kernels  46.3 us (100%)
    pallas_call x1, Pallas kernels, encoder(): pl.pallas_call(encoder_kernel, out_shape=(jax.ShapeDtypeStruct((cols_y, 8...  42.5 us
    pallas_call x1, Pallas kernels, decoder(): pl.pallas_call(decoder_kernel, out_shape=jax.ShapeDtypeStruct(shape, f32)...  3.84 us

profile of v6, /device:TPU:0, one launch (start us, length us, event | category | flops | bytes accessed | tf_op | source)
XLA Modules:
  0.0 46.3 jit_solution(13557730264902472654)
XLA Ops:
  0.0 42.5 %encoder.1 = (s32[4,8,128]{2,1,0:T(8,128)}, f32[4,2,32,128]{3,2,1,0:T(8,128)}, f32[2,4,64,128]{3,2,1,0:T(8,128)}) custom-call(s32[2,4]{1,0:T(2,128)} %owner_ref.1, s32[2,4]{1,0:T(2,128)} %local_ref.1, s32[2]{0:T(128)} %live_ref.1, bf16[32,256]{1,0:T(8,128)(2,1)} %features_ref.1, bf16[3,256]{1,0:T(4,128)(2,1)} %offsets_ref.1, s32[1,256]{1,0:T(1,128)} %bitcast.5, ...), custom_call_target="tpu_custom_call" | custom-call | tf_op jit(solution)/shard_map/encoder/pallas_call | solution.py:578
  42.5 3.8 %decoder.1 = f32[4,8,32,128]{3,2,1,0:T(8,128)} custom-call(s32[4,8,128]{2,1,0:T(8,128)} %get-tuple-element.8.codes_ref, f32[4,2,32,128]{3,2,1,0:T(8,128)} %get-tuple-element.9.held_ref, f32[2,4,64,128]{3,2,1,0:T(8,128)} %get-tuple-element.10.back_hbm, bf16[192,128]{1,0:T(8,128)(2,1)} %constant.11.clone.inverse_ref, bf16[32,32]{1,0:T(8,128)(2,1)} %w_point_ref.1, ...), custom_call_target="tpu_custom_call" | custom-call | tf_op jit(solution)/shard_map/decoder/pallas_call | solution.py:738
